TPU v7x, 32 devices: a whole 2x2x4 slice. The times are simulated.
32 devices in a mesh: groups: 2 (over x), space: 16 (over z, y, core).
Axes of the slice: x: 2, y: 2, z: 4, core: 2. Of those that a mesh axis runs over, the one named last changes fastest.
Arguments:
- field: bfloat16 [64, 256, 1024], P(('groups', 'space')), parts along dimension 0, may hold values from -3 to 3
- history: bfloat16 [3, 64, 1024], P(None, ('groups', 'space')), parts along dimension 1, may hold values from -3 to 3
- source: bfloat16 [64, 256, 1024], P(('groups', 'space')), parts along dimension 0, may hold values from -6 to 6
- row_conduct: float32 [2048], P('groups'), parts along dimension 0, may hold values from 0.25 to 2
- col_conduct: float32 [64, 1024], P(('groups', 'space')), parts along dimension 0, may hold values from 0.25 to 2
Outputs:
- spectrum: bfloat16 [64, 256, 1024], P('groups', 'space'), parts along dimension 0
There are 2 independent parts, one for each index of `groups`. A program takes and returns all parts, laid end to end along the dimension named above; each array names one. Nothing has to cross between parts.
All inputs are finite; a program needn't handle non-finite values.
Results may differ from a plain program's by a relative error of at most 0.0045.
Values may be sent and summed in bfloat16 or wider, within the bound.
No kernel may reach another device: no remote copies, remote signals or barrier semaphores. Data moves between devices by JAX's collectives and lax.ppermute only.
A program may use at most 64 MiB of HBM per device.

v0:
```python
import functools
import math

import jax
import jax.numpy as jnp
import numpy as np
from jax import lax
from jax.experimental import pallas as pl
from jax.experimental.pallas import tpu as pltpu
from jax.sharding import PartitionSpec as P

SWEEPS = 4
VMEM = pl.BlockSpec(memory_space=pltpu.VMEM)
SMEM = pl.BlockSpec(memory_space=pltpu.SMEM)


def slot_order(steps, devices):
    share = steps // devices
    order = []
    for core in range(2):
        for chip in range(devices // 2):
            first = (chip * 2 + core) * share
            order += list(range(first, first + share, 2)) + list(range(first + 1, first + share, 2))
    return np.array(order)


def transform_tables(steps, devices):
    index = np.arange(steps)
    freqs = np.where(index == 1, steps // 2, index // 2)
    use_cos = (index % 2 == 0) | (index == 1)
    phase = 2.0 * np.pi / steps * (freqs[:, None] * index[None, :] % steps)
    table = np.where(use_cos[:, None], np.cos(phase), -np.sin(phase)) / math.sqrt(steps)
    table = table[slot_order(steps, devices)]
    high = table.astype(jnp.bfloat16)
    low = (table - high.astype(np.float64)).astype(jnp.bfloat16)
    return high, low


def symbol_tables(steps):
    pair = np.arange(steps // 2)

    def real_part(freq):
        theta = 2.0 * np.pi / steps * freq
        return 11.0 / 6.0 - 3.0 * np.cos(theta) + 1.5 * np.cos(2.0 * theta) - np.cos(3.0 * theta) / 3.0

    theta = 2.0 * np.pi / steps * pair
    cross = 3.0 * np.sin(theta) - 1.5 * np.sin(2.0 * theta) + np.sin(3.0 * theta) / 3.0
    second = np.where(pair == 0, steps // 2, pair)
    return np.stack([real_part(pair), real_part(second), cross]).astype(np.float32)


def transform_kernel(
    outer, scal, field, halo, hist, source, row_c, col_c, high, low, own, other, r_high, r_low
):
    core, chip = scal[0], scal[1]
    row = core if outer else 1 - core
    beside = 1 - row
    steps, cols = r_high.shape
    rc = 0.5 * row_c[...]
    cc = 0.5 * col_c[pl.ds(row, 1)]
    cl = pltpu.roll(cc, 1, 1)
    diag = 2.0 * rc + cc + cl
    tile = 16

    def at(i, before):
        rows = pl.ds(pl.multiple_of(i * tile, tile), tile)
        c = field[row, rows, :].astype(jnp.float32)
        near = field[beside, rows, :].astype(jnp.float32) + halo[0, rows, :].astype(jnp.float32)
        seq = jnp.concatenate([before, c], axis=0)
        back = (
            11.0 / 6.0 * c
            - 3.0 * seq[7 : 7 + tile]
            + 1.5 * seq[6 : 6 + tile]
            - seq[5 : 5 + tile] / 3.0
        )
        flux = diag * c - rc * near - cc * pltpu.roll(c, cols - 1, 1) - cl * pltpu.roll(c, 1, 1)
        res = source[row, rows, :].astype(jnp.float32) - back - flux
        upper = res.astype(jnp.bfloat16)
        r_high[rows, :] = upper
        r_low[rows, :] = (res - upper.astype(jnp.float32)).astype(jnp.bfloat16)
        return c[tile - 8 :]

    lax.fori_loop(0, steps // tile, at, hist[row])
    half = steps // 2
    chips, share, _ = own.shape
    width = min(cols, 256)
    for ref, which in ((other, 1 - core), (own, core)):
        part = pl.ds(pl.multiple_of(which * half, half), half)
        for j in range(0, cols, width):
            a, b = r_high[:, j : j + width], r_low[:, j : j + width]
            acc = jnp.dot(high[part, :], a, preferred_element_type=jnp.float32)
            acc += jnp.dot(high[part, :], b, preferred_element_type=jnp.float32)
            acc += jnp.dot(low[part, :], a, preferred_element_type=jnp.float32)
            acc = acc.astype(jnp.bfloat16)
            for g in range(chips):
                ref[g ^ chip, :, j : j + width] = acc[g * share : (g + 1) * share]


def transform(outer, scal, field, halo, hist, source, row_c, col_c, tables, devices):
    _, steps, cols = field.shape
    shape = jax.ShapeDtypeStruct((devices // 2, steps // devices, cols), jnp.bfloat16)
    return pl.pallas_call(
        functools.partial(transform_kernel, outer),
        out_shape=(shape, shape),
        in_specs=[SMEM] + [VMEM] * 8,
        out_specs=(VMEM, VMEM),
        scratch_shapes=[pltpu.VMEM((steps, cols), jnp.bfloat16)] * 2,
        cost_estimate=pl.CostEstimate(
            flops=6 * steps * steps * cols, bytes_accessed=4 * steps * cols * 2, transcendentals=0
        ),
        name="transform",
    )(scal, field, halo, hist, source, row_c, col_c, *tables)


def assemble_kernel(own, other, *outs):
    for k, out in enumerate(outs):
        out[0] = own[k + 1]
        out[1] = other[k + 1]


def assemble(own, other):
    chips, share, cols = own.shape
    return pl.pallas_call(
        assemble_kernel,
        out_shape=[jax.ShapeDtypeStruct((2, share, cols), own.dtype)] * (chips - 1),
        in_specs=[VMEM] * 2,
        out_specs=[VMEM] * (chips - 1),
        cost_estimate=pl.CostEstimate(
            flops=0, bytes_accessed=4 * chips * share * cols * 2, transcendentals=0
        ),
        name="assemble",
    )(own, other)


def coefficient_kernel(scal, row_c, symbols, *refs):
    *faces, first, second, cross, ahead, behind = refs
    core, chip = scal[0], scal[1]
    rc = 0.5 * row_c[...]
    one, two, skew = symbols[0], symbols[1], symbols[2]
    for k, face in enumerate(faces):
        for j in range(4):
            side = core if j < 2 else 1 - core
            at = (chip ^ k) * 4 + side * 2 + j % 2
            cc = 0.5 * face[j : j + 1, :]
            cl = pltpu.roll(cc, 1, 1)
            diag = 2.0 * rc + cc + cl
            p0 = one + diag
            p1 = two + diag
            inverse = 1.0 / (p0 * p1 + skew * skew)
            first[at] = p1 * inverse
            second[at] = p0 * inverse
            cross[at] = skew * inverse
            ahead[at] = cc
            behind[at] = cl


def coefficients(scal, row_c, symbols, faces):
    rows = 4 * len(faces)
    pairs = symbols.shape[1]
    cols = row_c.shape[1]
    big = jax.ShapeDtypeStruct((rows, pairs, cols), jnp.float32)
    thin = jax.ShapeDtypeStruct((rows, 1, cols), jnp.float32)
    return pl.pallas_call(
        coefficient_kernel,
        out_shape=[big, big, big, thin, thin],
        in_specs=[SMEM] + [VMEM] * (2 + len(faces)),
        out_specs=[VMEM] * 5,
        cost_estimate=pl.CostEstimate(
            flops=10 * rows * pairs * cols, bytes_accessed=12 * rows * pairs * cols, transcendentals=0
        ),
        name="coefficients",
    )(scal, row_c, symbols, *faces)


def sweep_kernel(scal, row_c, first, second, cross, ahead, behind, *refs):
    *blocks, out, rhs_re, rhs_im, a_re, a_im, b_re, b_im, mixed = refs
    core, chip = scal[0], scal[1]
    rows, pairs, cols = rhs_re.shape
    chips = rows // 4
    rc = 0.5 * row_c[...]

    def solve(i, t0, t1):
        s = cross[i]
        return first[i] * t0 + s * t1, second[i] * t1 - s * t0

    def enter(block, k, side, outer):
        owner = core if side == 0 else 1 - core
        row = owner if outer else 1 - owner
        i = (chip ^ k) * 4 + owner * 2 + row
        both = block.astype(jnp.float32)
        t0, t1 = both[:pairs], both[pairs:]
        rhs_re[i], rhs_im[i] = t0, t1
        a_re[i], a_im[i] = solve(i, t0, t1)

    per = chips + 1
    for outer in (False, True):
        own, other, *far = blocks[per * outer : per * (outer + 1)]
        enter(own[0], 0, 0, outer)
        enter(other[0], 0, 1, outer)
        for k, block in enumerate(far):
            enter(block[0], k + 1, 0, outer)
            enter(block[1], k + 1, 1, outer)

    def neighbours(z, i, up, down):
        c = z[i]
        return (
            rc * (z[up] + z[down])
            + ahead[i] * pltpu.roll(c, cols - 1, 1)
            + behind[i] * pltpu.roll(c, 1, 1)
        )

    def sweep(src, dst):
        def at(i, carry):
            up = jnp.where(i == 0, rows - 1, i - 1)
            down = jnp.where(i == rows - 1, 0, i + 1)
            t0 = rhs_re[i] + neighbours(src[0], i, up, down)
            t1 = rhs_im[i] + neighbours(src[1], i, up, down)
            z0, z1 = solve(i, t0, t1)
            if dst is None:
                for j in range(mixed.shape[0]):
                    lanes = slice(j * 128, (j + 1) * 128)
                    mixed[j, pl.ds(0, pairs, stride=2), :] = z0[:, lanes]
                    mixed[j, pl.ds(1, pairs, stride=2), :] = z1[:, lanes]
                    out[i, :, lanes] = mixed[j].astype(out.dtype)
            else:
                dst[0][i], dst[1][i] = z0, z1
            return carry

        lax.fori_loop(0, rows, at, 0)

    src, dst = (a_re, a_im), (b_re, b_im)
    for step in range(SWEEPS - 1):
        sweep(src, None if step == SWEEPS - 2 else dst)
        src, dst = dst, src


def sweeps(scal, row_c, coeffs, blocks):
    rows, pairs, cols = coeffs[0].shape
    return pl.pallas_call(
        sweep_kernel,
        out_shape=jax.ShapeDtypeStruct((rows, 2 * pairs, cols), jnp.bfloat16),
        in_specs=[SMEM] + [VMEM] * (6 + len(blocks)),
        out_specs=VMEM,
        scratch_shapes=[pltpu.VMEM((rows, pairs, cols), jnp.float32)] * 6
        + [pltpu.VMEM((cols // 128, 2 * pairs, 128), jnp.float32)],
        cost_estimate=pl.CostEstimate(
            flops=80 * rows * pairs * cols, bytes_accessed=60 * rows * pairs * cols, transcendentals=0
        ),
        name="sweeps",
    )(scal, row_c, *coeffs, *blocks)


def on_device(field, history, source, row_conduct, col_conduct):
    devices = lax.axis_size("space")
    steps, cols = field.shape[1:]
    me = lax.axis_index("space")
    core, chip = me % 2, me // 2
    scal = jnp.stack([core, chip]).astype(jnp.int32)
    row_c = row_conduct.reshape(1, cols)
    partner = [(i, i ^ 1) for i in range(devices)]
    across = [(i, (i - 1 if i % 2 == 0 else i + 1) % devices) for i in range(devices)]

    def between(x, k):
        return lax.ppermute(x, "space", [(i, i ^ (2 * k)) for i in range(devices)])

    far_halo = lax.ppermute(lax.dynamic_slice_in_dim(field, core, 1, 0), "space", across)
    near_halo = lax.ppermute(lax.dynamic_slice_in_dim(field, 1 - core, 1, 0), "space", partner)
    face = jnp.concatenate([col_conduct, lax.ppermute(col_conduct, "space", partner)], axis=0)
    tables = transform_tables(steps, devices)
    earlier = jnp.pad(
        jnp.transpose(history, (1, 0, 2)).astype(jnp.float32), ((0, 0), (5, 0), (0, 0))
    )

    blocks = []
    faces = [face]
    for outer, halo in ((False, near_halo), (True, far_halo)):
        own, other = transform(
            outer, scal, field, halo, earlier, source, row_c, col_conduct, tables, devices
        )
        other = lax.ppermute(other, "space", partner)
        packs = assemble(own, other)
        blocks += [own, other] + [between(pack, k + 1) for k, pack in enumerate(packs)]
        if not outer:
            faces += [between(face, k) for k in range(1, devices // 2)]
    pairs = steps // devices // 2
    symbols = lax.dynamic_slice_in_dim(jnp.asarray(symbol_tables(steps)), me * pairs, pairs, 1)
    coeffs = coefficients(scal, row_c, symbols[:, :, None], faces)
    return sweeps(scal, row_c, coeffs, blocks)


def solution(mesh):
    in_specs = (
        P(("groups", "space"), None, None),
        P(None, ("groups", "space"), None),
        P(("groups", "space"), None, None),
        P("groups"),
        P(("groups", "space"), None),
    )
    out_specs = P("groups", "space", None)
    return jax.shard_map(
        on_device, mesh=mesh, in_specs=in_specs, out_specs=out_specs, check_vma=False
    )
```

profile of v0, /device:TPU:0, one launch (start us, length us, event | category | flops | bytes accessed | tf_op | source)
XLA Modules:
  0.0 91.4 jit_solution(2782319743257006457)
XLA Ops:
  0.0 1.3 %constant_dynamic-slice_fusion = (bf16[1,256,1024]{2,1,0:T(8,128)(2,1)S(1)}, bf16[1,256,1024]{2,1,0:T(8,128)(2,1)S(1)}) fusion(bf16[2,256,1024]{2,1,0:T(8,128)(2,1)} %field.3, s32[]{:T(128)S(6)} %select_n.24, s32[]{:T(128)S(6)} %select_n.23), kind=kLoop, calls=%fused_computation.4 | loop fusion | bytes 2097160 | tf_op jit(solution)/shard_map/dynamic_slice | solution.py:266
  1.3 0.0 copy-start.27
  1.3 5.5 %collective-permute-start.17 = (bf16[1,256,1024]{2,1,0:T(8,128)(2,1)S(1)}, bf16[1,256,1024]{2,1,0:T(8,128)(2,1)S(1)}, u32[]{:S(2)}, u32[]{:S(2)}) collective-permute-start(bf16[1,256,1024]{2,1,0:T(8,128)(2,1)S(1)} %get-tuple-element.51), channel_id=1, source_target_pairs={{0,15},{1,2},{2,1},{3,4},{4,3},{5,6},{6,5},{7,8},{8,7},{9,10},{10,... | collective-permute-start | bytes 1572872 | tf_op jit(solution)/shard_map/ppermute | solution.py:266
  6.8 0.0 collective-permute-start.8
  6.8 0.6 pad_add_fusion.scal
  7.5 0.6 pad_convert_fusion.hist
  8.1 5.7 %collective-permute-done.17.halo = bf16[1,256,1024]{2,1,0:T(8,128)(2,1)S(1)} collective-permute-done((bf16[1,256,1024]{2,1,0:T(8,128)(2,1)S(1)}, bf16[1,256,1024]{2,1,0:T(8,128)(2,1)S(1)}, u32[]{:S(2)}, u32[]{:S(2)}) %collective-permute-start.17) | collective-permute-done | bytes 524320 | tf_op jit(solution)/shard_map/ppermute | solution.py:266
  13.8 0.8 copy-done.3
  14.6 4.9 %transform.3 = (bf16[8,16,1024]{2,1,0:T(8,128)(2,1)}, bf16[8,16,1024]{2,1,0:T(8,128)(2,1)}) custom-call(s32[2]{0:T(128)} %pad_add_fusion.scal, bf16[2,256,1024]{2,1,0:T(8,128)(2,1)} %field.3, bf16[1,256,1024]{2,1,0:T(8,128)(2,1)} %copy-done.3, f32[2,8,1024]{2,1,0:T(8,128)} %pad_convert_fusion.hist, bf16[2,256,1024]{2,1,0:T(8,128)(2,1)} %source.3, ...), custom_call_target="tpu_custom_call" | custom-call | flops 402653184 | bytes 2097152 | tf_op jit(solution)/shard_map/transform/pallas_call | solution.py:102
  19.5 3.2 %collective-permute-start.18 = (bf16[8,16,1024]{2,1,0:T(8,128)(2,1)}, bf16[8,16,1024]{2,1,0:T(8,128)(2,1)S(1)}, u32[]{:S(2)}, u32[]{:S(2)}) collective-permute-start(bf16[8,16,1024]{2,1,0:T(8,128)(2,1)} %get-tuple-element.43), channel_id=1, source_target_pairs={{0,1},{1,0},{2,3},{3,2},{4,5},{5,4},{6,7},{7,6},{8,9},{9,8},{10,11... | collective-permute-start | bytes 786440 | tf_op jit(solution)/shard_map/ppermute | solution.py:280
  22.7 0.8 copy-done.2
  23.5 5.0 %transform.2 = (bf16[8,16,1024]{2,1,0:T(8,128)(2,1)}, bf16[8,16,1024]{2,1,0:T(8,128)(2,1)}) custom-call(s32[2]{0:T(128)} %pad_add_fusion.scal, bf16[2,256,1024]{2,1,0:T(8,128)(2,1)} %field.3, bf16[1,256,1024]{2,1,0:T(8,128)(2,1)} %copy-done.2, f32[2,8,1024]{2,1,0:T(8,128)} %pad_convert_fusion.hist, bf16[2,256,1024]{2,1,0:T(8,128)(2,1)} %source.3, ...), custom_call_target="tpu_custom_call" | custom-call | flops 402653184 | bytes 2097152 | tf_op jit(solution)/shard_map/transform/pallas_call | solution.py:102
  28.5 0.0 collective-permute-start.9
  28.5 0.5 collective-permute-start
  29.0 1.2 %collective-permute-done = f32[2,1024]{1,0:T(2,128)S(1)} collective-permute-done((f32[2,1024]{1,0:T(2,128)S(1)}, f32[2,1024]{1,0:T(2,128)S(1)}, u32[]{:S(2)}, u32[]{:S(2)}) %collective-permute-start) | collective-permute-done | bytes 8224 | tf_op jit(solution)/shard_map/ppermute | solution.py:268
  30.2 4.9 %collective-permute-start.7 = (f32[4,1024]{1,0:T(4,128)S(1)}, f32[4,1024]{1,0:T(4,128)S(1)}, u32[]{:S(2)}, u32[]{:S(2)}) collective-permute-start(f32[4,1024]{1,0:T(4,128)S(1)} %pad_maximum_fusion.refs_0_), channel_id=1, source_target_pairs={{0,14},{1,15},{2,12},{3,13},{4,10},{5,11},{6,8},{7,9},{8,6},{9,7},... | collective-permute-start | bytes 49160 | tf_op jit(solution)/shard_map/ppermute | solution.py:264
  35.1 0.2 collective-permute-start.6
  35.3 0.5 collective-permute-start.5
  35.8 1.0 %collective-permute-done.7.refs_7_ = f32[4,1024]{1,0:T(4,128)S(1)} collective-permute-done((f32[4,1024]{1,0:T(4,128)S(1)}, f32[4,1024]{1,0:T(4,128)S(1)}, u32[]{:S(2)}, u32[]{:S(2)}) %collective-permute-start.7) | collective-permute-done | bytes 16416 | tf_op jit(solution)/shard_map/ppermute | solution.py:264
  36.8 1.3 %collective-permute-start.4 = (f32[4,1024]{1,0:T(4,128)S(1)}, f32[4,1024]{1,0:T(4,128)S(1)}, u32[]{:S(2)}, u32[]{:S(2)}) collective-permute-start(f32[4,1024]{1,0:T(4,128)S(1)} %pad_maximum_fusion.refs_0_), channel_id=1, source_target_pairs={{0,8},{1,9},{2,10},{3,11},{4,12},{5,13},{6,14},{7,15},{8,0},{9,1},... | collective-permute-start | bytes 49160 | tf_op jit(solution)/shard_map/ppermute | solution.py:264
  38.1 2.5 %collective-permute-done.6.refs_6_ = f32[4,1024]{1,0:T(4,128)S(1)} collective-permute-done((f32[4,1024]{1,0:T(4,128)S(1)}, f32[4,1024]{1,0:T(4,128)S(1)}, u32[]{:S(2)}, u32[]{:S(2)}) %collective-permute-start.6) | collective-permute-done | bytes 16416 | tf_op jit(solution)/shard_map/ppermute | solution.py:264
  40.6 1.5 %collective-permute-start.3 = (f32[4,1024]{1,0:T(4,128)S(1)}, f32[4,1024]{1,0:T(4,128)S(1)}, u32[]{:S(2)}, u32[]{:S(2)}) collective-permute-start(f32[4,1024]{1,0:T(4,128)S(1)} %pad_maximum_fusion.refs_0_), channel_id=1, source_target_pairs={{0,6},{1,7},{2,4},{3,5},{4,2},{5,3},{6,0},{7,1},{8,14},{9,15},{10,... | collective-permute-start | bytes 49160 | tf_op jit(solution)/shard_map/ppermute | solution.py:264
  42.1 0.3 collective-permute-start.2
  42.4 0.5 copy-done
  42.8 1.8 %assemble.3 = (bf16[2,16,1024]{2,1,0:T(8,128)(2,1)}, bf16[2,16,1024]{2,1,0:T(8,128)(2,1)}, bf16[2,16,1024]{2,1,0:T(8,128)(2,1)}, bf16[2,16,1024]{2,1,0:T(8,128)(...) custom-call(bf16[8,16,1024]{2,1,0:T(8,128)(2,1)} %get-tuple-element.42.own.refs_9_, ...), custom_call_target="tpu_custom_call" | custom-call | bytes 1048576 | tf_op jit(solution)/shard_map/assemble/pallas_call | solution.py:123
  44.7 1.4 %collective-permute-start.19 = (bf16[2,16,1024]{2,1,0:T(8,128)(2,1)}, bf16[2,16,1024]{2,1,0:T(8,128)(2,1)S(1)}, u32[]{:S(2)}, u32[]{:S(2)}) collective-permute-start(bf16[2,16,1024]{2,1,0:T(8,128)(2,1)} %get-tuple-element.44), channel_id=1, source_target_pairs={{0,2},{1,3},{2,0},{3,1},{4,6},{5,7},{6,4},{7,5},{8,10},{9,11},{10,... | collective-permute-start | bytes 196616 | tf_op jit(solution)/shard_map/ppermute | solution.py:264
  46.0 0.0 collective-permute-done.4.refs_4_
  46.0 0.7 collective-permute-start.20
  46.7 0.0 collective-permute-done.3.refs_3_
  46.7 1.5 %collective-permute-start.21 = (bf16[2,16,1024]{2,1,0:T(8,128)(2,1)}, bf16[2,16,1024]{2,1,0:T(8,128)(2,1)S(1)}, u32[]{:S(2)}, u32[]{:S(2)}) collective-permute-start(bf16[2,16,1024]{2,1,0:T(8,128)(2,1)} %get-tuple-element.46), channel_id=1, source_target_pairs={{0,6},{1,7},{2,4},{3,5},{4,2},{5,3},{6,0},{7,1},{8,14},{9,15},{10,... | collective-permute-start | bytes 196616 | tf_op jit(solution)/shard_map/ppermute | solution.py:264
  48.2 1.2 %collective-permute-start.22 = (bf16[2,16,1024]{2,1,0:T(8,128)(2,1)}, bf16[2,16,1024]{2,1,0:T(8,128)(2,1)S(1)}, u32[]{:S(2)}, u32[]{:S(2)}) collective-permute-start(bf16[2,16,1024]{2,1,0:T(8,128)(2,1)} %get-tuple-element.47), channel_id=1, source_target_pairs={{0,8},{1,9},{2,10},{3,11},{4,12},{5,13},{6,14},{7,15},{8,0},{9,1},... | collective-permute-start | bytes 196616 | tf_op jit(solution)/shard_map/ppermute | solution.py:264
  49.4 0.0 collective-permute-done.9.other.refs_1_
  49.4 0.3 collective-permute-start.1
  49.8 0.4 copy-done.1
  50.2 1.8 %assemble.2 = (bf16[2,16,1024]{2,1,0:T(8,128)(2,1)}, bf16[2,16,1024]{2,1,0:T(8,128)(2,1)}, bf16[2,16,1024]{2,1,0:T(8,128)(2,1)}, bf16[2,16,1024]{2,1,0:T(8,128)(...) custom-call(bf16[8,16,1024]{2,1,0:T(8,128)(2,1)} %get-tuple-element.33.own.refs_0_, ...), custom_call_target="tpu_custom_call" | custom-call | bytes 1048576 | tf_op jit(solution)/shard_map/assemble/pallas_call | solution.py:123
  52.0 1.2 %collective-permute-done.1.refs_1_ = f32[4,1024]{1,0:T(4,128)S(1)} collective-permute-done((f32[4,1024]{1,0:T(4,128)S(1)}, f32[4,1024]{1,0:T(4,128)S(1)}, u32[]{:S(2)}, u32[]{:S(2)}) %collective-permute-start.1) | collective-permute-done | bytes 16416 | tf_op jit(solution)/shard_map/ppermute | solution.py:264
  53.3 2.5 %collective-permute-start.23 = (bf16[2,16,1024]{2,1,0:T(8,128)(2,1)S(1)}, bf16[2,16,1024]{2,1,0:T(8,128)(2,1)S(1)}, u32[]{:S(2)}, u32[]{:S(2)}) collective-permute-start(bf16[2,16,1024]{2,1,0:T(8,128)(2,1)S(1)} %copy-done.31), channel_id=1, source_target_pairs={{0,10},{1,11},{2,8},{3,9},{4,14},{5,15},{6,12},{7,13},{8,2},{9,3},... | collective-permute-start | bytes 196616 | tf_op jit(solution)/shard_map/ppermute | solution.py:264
  55.7 0.0 collective-permute-done.19.refs_11_
  55.7 1.0 %collective-permute-start.24 = (bf16[2,16,1024]{2,1,0:T(8,128)(2,1)S(1)}, bf16[2,16,1024]{2,1,0:T(8,128)(2,1)S(1)}, u32[]{:S(2)}, u32[]{:S(2)}) collective-permute-start(bf16[2,16,1024]{2,1,0:T(8,128)(2,1)S(1)} %copy-done.30), channel_id=1, source_target_pairs={{0,12},{1,13},{2,14},{3,15},{4,8},{5,9},{6,10},{7,11},{8,4},{9,5},... | collective-permute-start | bytes 196616 | tf_op jit(solution)/shard_map/ppermute | solution.py:264
  56.7 3.1 %collective-permute-start.25 = (bf16[2,16,1024]{2,1,0:T(8,128)(2,1)S(1)}, bf16[2,16,1024]{2,1,0:T(8,128)(2,1)S(1)}, u32[]{:S(2)}, u32[]{:S(2)}) collective-permute-start(bf16[2,16,1024]{2,1,0:T(8,128)(2,1)S(1)} %copy-done.29), channel_id=1, source_target_pairs={{0,14},{1,15},{2,12},{3,13},{4,10},{5,11},{6,8},{7,9},{8,6},{9,7},... | collective-permute-start | bytes 196616 | tf_op jit(solution)/shard_map/ppermute | solution.py:264
  59.8 1.3 %collective-permute-start.10 = (bf16[2,16,1024]{2,1,0:T(8,128)(2,1)}, bf16[2,16,1024]{2,1,0:T(8,128)(2,1)S(1)}, u32[]{:S(2)}, u32[]{:S(2)}) collective-permute-start(bf16[2,16,1024]{2,1,0:T(8,128)(2,1)} %get-tuple-element.35), channel_id=1, source_target_pairs={{0,2},{1,3},{2,0},{3,1},{4,6},{5,7},{6,4},{7,5},{8,10},{9,11},{10,... | collective-permute-start | bytes 196616 | tf_op jit(solution)/shard_map/ppermute | solution.py:264
  61.1 0.0 collective-permute-done.22.refs_14_
  61.2 0.0 collective-permute-start.11
  61.2 0.0 collective-permute-done.23.refs_15_
  61.2 2.1 %collective-permute-start.12 = (bf16[2,16,1024]{2,1,0:T(8,128)(2,1)}, bf16[2,16,1024]{2,1,0:T(8,128)(2,1)S(1)}, u32[]{:S(2)}, u32[]{:S(2)}) collective-permute-start(bf16[2,16,1024]{2,1,0:T(8,128)(2,1)} %get-tuple-element.37), channel_id=1, source_target_pairs={{0,6},{1,7},{2,4},{3,5},{4,2},{5,3},{6,0},{7,1},{8,14},{9,15},{10,... | collective-permute-start | bytes 196616 | tf_op jit(solution)/shard_map/ppermute | solution.py:264
  63.3 0.6 collective-permute-start.13
  63.9 0.3 collective-permute-done.25.refs_17_
  64.2 2.8 %collective-permute-start.14 = (bf16[2,16,1024]{2,1,0:T(8,128)(2,1)}, bf16[2,16,1024]{2,1,0:T(8,128)(2,1)S(1)}, u32[]{:S(2)}, u32[]{:S(2)}) collective-permute-start(bf16[2,16,1024]{2,1,0:T(8,128)(2,1)} %get-tuple-element.39), channel_id=1, source_target_pairs={{0,10},{1,11},{2,8},{3,9},{4,14},{5,15},{6,12},{7,13},{8,2},{9,3},... | collective-permute-start | bytes 196616 | tf_op jit(solution)/shard_map/ppermute | solution.py:264
  67.0 0.0 collective-permute-done.10.refs_2_
  67.0 0.9 %collective-permute-start.15 = (bf16[2,16,1024]{2,1,0:T(8,128)(2,1)}, bf16[2,16,1024]{2,1,0:T(8,128)(2,1)S(1)}, u32[]{:S(2)}, u32[]{:S(2)}) collective-permute-start(bf16[2,16,1024]{2,1,0:T(8,128)(2,1)} %get-tuple-element.40), channel_id=1, source_target_pairs={{0,12},{1,13},{2,14},{3,15},{4,8},{5,9},{6,10},{7,11},{8,4},{9,5},... | collective-permute-start | bytes 196616 | tf_op jit(solution)/shard_map/ppermute | solution.py:264
  67.9 0.0 collective-permute-done.11.refs_3_
  68.0 3.8 %collective-permute-start.16 = (bf16[2,16,1024]{2,1,0:T(8,128)(2,1)}, bf16[2,16,1024]{2,1,0:T(8,128)(2,1)S(1)}, u32[]{:S(2)}, u32[]{:S(2)}) collective-permute-start(bf16[2,16,1024]{2,1,0:T(8,128)(2,1)} %get-tuple-element.41), channel_id=1, source_target_pairs={{0,14},{1,15},{2,12},{3,13},{4,10},{5,11},{6,8},{7,9},{8,6},{9,7},... | collective-permute-start | bytes 196616 | tf_op jit(solution)/shard_map/ppermute | solution.py:264
  71.7 0.1 dynamic-slice_bitcast_fusion
  71.8 0.7 copy.9.symbols
  72.5 3.1 %coefficients.1 = (f32[32,8,1024]{2,1,0:T(8,128)}, f32[32,8,1024]{2,1,0:T(8,128)}, f32[32,8,1024]{2,1,0:T(8,128)}, f32[32,1,1024]{2,1,0:T(1,128)}, f32[32,1,1024]{2,1,0:T(1,128)}) custom-call(s32[2]{0:T(128)} %pad_add_fusion.scal, f32[1,1024]{1,0:T(1,128)} %bitcast.11, f32[3,8,1]{2,1,0:T(8,128)} %copy.9.symbols, f32[4,1024]{1,0:T(4,128)} %copy-done.19, ...), custom_call_target="tpu_custom_call" | custom-call | flops 2621440 | bytes 3145728 | tf_op jit(solution)/shard_map/coefficients/pallas_call | solution.py:163
  75.6 0.0 collective-permute-done.12.refs_4_
  75.6 0.0 collective-permute-done.13.refs_5_
  75.7 0.0 collective-permute-done.16.refs_8_
  75.8 0.5 copy-done.14
  76.2 0.0 copy-done.15
  76.3 0.0 copy-done.16
  76.3 0.0 copy-done.17
  76.3 0.0 copy-done.18
  76.4 15.1 %sweeps.1 = bf16[32,16,1024]{2,1,0:T(8,128)(2,1)} custom-call(s32[2]{0:T(128)} %pad_add_fusion.scal, f32[1,1024]{1,0:T(1,128)} %bitcast.12, f32[32,8,1024]{2,1,0:T(8,128)} %get-tuple-element.28.first, f32[32,8,1024]{2,1,0:T(8,128)} %get-tuple-element.29.second, f32[32,8,1024]{2,1,0:T(8,128)} %get-tuple-element.30.cross, ...), custom_call_target="tpu_custom_call" | custom-call | flops 20971520 | bytes 15728640 | tf_op jit(solution)/shard_map/sweeps/pallas_call | solution.py:239
  (65 shorter events, 0.1 us)
Async XLA Ops:
  1.3 5.6 %copy-start.27 = (bf16[3,2,1024]{2,1,0:T(2,128)(2,1)S(1)}, bf16[3,2,1024]{2,1,0:T(2,128)(2,1)}, u32[]{:S(2)}) copy-start(bf16[3,2,1024]{2,1,0:T(2,128)(2,1)} %param.9) | copy-start | bytes 36868
  1.3 12.5 %collective-permute-start.17 = (bf16[1,256,1024]{2,1,0:T(8,128)(2,1)S(1)}, bf16[1,256,1024]{2,1,0:T(8,128)(2,1)S(1)}, u32[]{:S(2)}, u32[]{:S(2)}) collective-permute-start(bf16[1,256,1024]{2,1,0:T(8,128)(2,1)S(1)} %get-tuple-element.51), channel_id=1, source_target_pairs={{0,15},{1,2},{2,1},{3,4},{4,3},{5,6},{6,5},{7,8},{8,7},{9,10},{10,... | collective-permute-start | bytes 1572872 | tf_op jit(solution)/shard_map/ppermute | solution.py:266
  6.8 15.9 %collective-permute-start.8 = (bf16[1,256,1024]{2,1,0:T(8,128)(2,1)S(1)}, bf16[1,256,1024]{2,1,0:T(8,128)(2,1)S(1)}, u32[]{:S(2)}, u32[]{:S(2)}) collective-permute-start(bf16[1,256,1024]{2,1,0:T(8,128)(2,1)S(1)} %get-tuple-element.52), channel_id=1, source_target_pairs={{0,1},{1,0},{2,3},{3,2},{4,5},{5,4},{6,7},{7,6},{8,9},{9,8},{10,11... | collective-permute-start | bytes 1572872 | tf_op jit(solution)/shard_map/ppermute | solution.py:267
  13.8 0.8 copy-start.3
  19.5 8.9 %copy-start.4 = (f32[2,1024]{1,0:T(2,128)S(1)}, f32[2,1024]{1,0:T(2,128)}, u32[]{:S(2)}) copy-start(f32[2,1024]{1,0:T(2,128)} %col_c.3) | copy-start | bytes 24580
  19.5 22.6 %collective-permute-start.18 = (bf16[8,16,1024]{2,1,0:T(8,128)(2,1)}, bf16[8,16,1024]{2,1,0:T(8,128)(2,1)S(1)}, u32[]{:S(2)}, u32[]{:S(2)}) collective-permute-start(bf16[8,16,1024]{2,1,0:T(8,128)(2,1)} %get-tuple-element.43), channel_id=1, source_target_pairs={{0,1},{1,0},{2,3},{3,2},{4,5},{5,4},{6,7},{7,6},{8,9},{9,8},{10,11... | collective-permute-start | bytes 786440 | tf_op jit(solution)/shard_map/ppermute | solution.py:280
  22.7 0.8 copy-start.2
  28.5 21.0 %collective-permute-start.9 = (bf16[8,16,1024]{2,1,0:T(8,128)(2,1)}, bf16[8,16,1024]{2,1,0:T(8,128)(2,1)S(1)}, u32[]{:S(2)}, u32[]{:S(2)}) collective-permute-start(bf16[8,16,1024]{2,1,0:T(8,128)(2,1)} %get-tuple-element.34), channel_id=1, source_target_pairs={{0,1},{1,0},{2,3},{3,2},{4,5},{5,4},{6,7},{7,6},{8,9},{9,8},{10,11... | collective-permute-start | bytes 786440 | tf_op jit(solution)/shard_map/ppermute | solution.py:280
  28.5 1.7 %collective-permute-start = (f32[2,1024]{1,0:T(2,128)S(1)}, f32[2,1024]{1,0:T(2,128)S(1)}, u32[]{:S(2)}, u32[]{:S(2)}) collective-permute-start(f32[2,1024]{1,0:T(2,128)S(1)} %copy-done.4), channel_id=1, source_target_pairs={{0,1},{1,0},{2,3},{3,2},{4,5},{5,4},{6,7},{7,6},{8,9},{9,8},{10,11... | collective-permute-start | bytes 24584 | tf_op jit(solution)/shard_map/ppermute | solution.py:268
  30.2 19.2 %copy-start.19 = (f32[4,1024]{1,0:T(4,128)}, f32[4,1024]{1,0:T(4,128)S(1)}, u32[]{:S(2)}) copy-start(f32[4,1024]{1,0:T(4,128)S(1)} %pad_maximum_fusion.refs_0_) | copy-start | bytes 49156
  30.2 6.6 %collective-permute-start.7 = (f32[4,1024]{1,0:T(4,128)S(1)}, f32[4,1024]{1,0:T(4,128)S(1)}, u32[]{:S(2)}, u32[]{:S(2)}) collective-permute-start(f32[4,1024]{1,0:T(4,128)S(1)} %pad_maximum_fusion.refs_0_), channel_id=1, source_target_pairs={{0,14},{1,15},{2,12},{3,13},{4,10},{5,11},{6,8},{7,9},{8,6},{9,7},... | collective-permute-start | bytes 49160 | tf_op jit(solution)/shard_map/ppermute | solution.py:264
  35.1 5.5 %collective-permute-start.6 = (f32[4,1024]{1,0:T(4,128)S(1)}, f32[4,1024]{1,0:T(4,128)S(1)}, u32[]{:S(2)}, u32[]{:S(2)}) collective-permute-start(f32[4,1024]{1,0:T(4,128)S(1)} %pad_maximum_fusion.refs_0_), channel_id=1, source_target_pairs={{0,12},{1,13},{2,14},{3,15},{4,8},{5,9},{6,10},{7,11},{8,4},{9,5},... | collective-permute-start | bytes 49160 | tf_op jit(solution)/shard_map/ppermute | solution.py:264
  35.3 9.3 %collective-permute-start.5 = (f32[4,1024]{1,0:T(4,128)S(1)}, f32[4,1024]{1,0:T(4,128)S(1)}, u32[]{:S(2)}, u32[]{:S(2)}) collective-permute-start(f32[4,1024]{1,0:T(4,128)S(1)} %pad_maximum_fusion.refs_0_), channel_id=1, source_target_pairs={{0,10},{1,11},{2,8},{3,9},{4,14},{5,15},{6,12},{7,13},{8,2},{9,3},... | collective-permute-start | bytes 49160 | tf_op jit(solution)/shard_map/ppermute | solution.py:264
  36.8 7.8 %copy-start.20 = (f32[4,1024]{1,0:T(4,128)}, f32[4,1024]{1,0:T(4,128)S(1)}, u32[]{:S(2)}) copy-start(f32[4,1024]{1,0:T(4,128)S(1)} %collective-permute-done.7.refs_7_) | copy-start | bytes 49156
  36.8 9.2 %collective-permute-start.4 = (f32[4,1024]{1,0:T(4,128)S(1)}, f32[4,1024]{1,0:T(4,128)S(1)}, u32[]{:S(2)}, u32[]{:S(2)}) collective-permute-start(f32[4,1024]{1,0:T(4,128)S(1)} %pad_maximum_fusion.refs_0_), channel_id=1, source_target_pairs={{0,8},{1,9},{2,10},{3,11},{4,12},{5,13},{6,14},{7,15},{8,0},{9,1},... | collective-permute-start | bytes 49160 | tf_op jit(solution)/shard_map/ppermute | solution.py:264
  40.6 4.0 %copy-start.21 = (f32[4,1024]{1,0:T(4,128)}, f32[4,1024]{1,0:T(4,128)S(1)}, u32[]{:S(2)}) copy-start(f32[4,1024]{1,0:T(4,128)S(1)} %collective-permute-done.6.refs_6_) | copy-start | bytes 49156
  40.6 6.1 %collective-permute-start.3 = (f32[4,1024]{1,0:T(4,128)S(1)}, f32[4,1024]{1,0:T(4,128)S(1)}, u32[]{:S(2)}, u32[]{:S(2)}) collective-permute-start(f32[4,1024]{1,0:T(4,128)S(1)} %pad_maximum_fusion.refs_0_), channel_id=1, source_target_pairs={{0,6},{1,7},{2,4},{3,5},{4,2},{5,3},{6,0},{7,1},{8,14},{9,15},{10,... | collective-permute-start | bytes 49160 | tf_op jit(solution)/shard_map/ppermute | solution.py:264
  42.1 0.7 copy-start
  42.1 6.1 %collective-permute-start.2 = (f32[4,1024]{1,0:T(4,128)S(1)}, f32[4,1024]{1,0:T(4,128)S(1)}, u32[]{:S(2)}, u32[]{:S(2)}) collective-permute-start(f32[4,1024]{1,0:T(4,128)S(1)} %pad_maximum_fusion.refs_0_), channel_id=1, source_target_pairs={{0,4},{1,5},{2,6},{3,7},{4,0},{5,1},{6,2},{7,3},{8,12},{9,13},{10,... | collective-permute-start | bytes 49160 | tf_op jit(solution)/shard_map/ppermute | solution.py:264
  44.6 7.4 %copy-start.22 = (f32[4,1024]{1,0:T(4,128)}, f32[4,1024]{1,0:T(4,128)S(1)}, u32[]{:S(2)}) copy-start(f32[4,1024]{1,0:T(4,128)S(1)} %collective-permute-done.5.refs_5_) | copy-start | bytes 49156
  44.7 11.1 %collective-permute-start.19 = (bf16[2,16,1024]{2,1,0:T(8,128)(2,1)}, bf16[2,16,1024]{2,1,0:T(8,128)(2,1)S(1)}, u32[]{:S(2)}, u32[]{:S(2)}) collective-permute-start(bf16[2,16,1024]{2,1,0:T(8,128)(2,1)} %get-tuple-element.44), channel_id=1, source_target_pairs={{0,2},{1,3},{2,0},{3,1},{4,6},{5,7},{6,4},{7,5},{8,10},{9,11},{10,... | collective-permute-start | bytes 196616 | tf_op jit(solution)/shard_map/ppermute | solution.py:264
  46.0 6.0 %copy-start.23 = (f32[4,1024]{1,0:T(4,128)}, f32[4,1024]{1,0:T(4,128)S(1)}, u32[]{:S(2)}) copy-start(f32[4,1024]{1,0:T(4,128)S(1)} %collective-permute-done.4.refs_4_) | copy-start | bytes 49156
  46.0 10.7 %collective-permute-start.20 = (bf16[2,16,1024]{2,1,0:T(8,128)(2,1)}, bf16[2,16,1024]{2,1,0:T(8,128)(2,1)S(1)}, u32[]{:S(2)}, u32[]{:S(2)}) collective-permute-start(bf16[2,16,1024]{2,1,0:T(8,128)(2,1)} %get-tuple-element.45), channel_id=1, source_target_pairs={{0,4},{1,5},{2,6},{3,7},{4,0},{5,1},{6,2},{7,3},{8,12},{9,13},{10,... | collective-permute-start | bytes 196616 | tf_op jit(solution)/shard_map/ppermute | solution.py:264
  46.7 5.3 %copy-start.24 = (f32[4,1024]{1,0:T(4,128)}, f32[4,1024]{1,0:T(4,128)S(1)}, u32[]{:S(2)}) copy-start(f32[4,1024]{1,0:T(4,128)S(1)} %collective-permute-done.3.refs_3_) | copy-start | bytes 49156
  46.7 13.1 %collective-permute-start.21 = (bf16[2,16,1024]{2,1,0:T(8,128)(2,1)}, bf16[2,16,1024]{2,1,0:T(8,128)(2,1)S(1)}, u32[]{:S(2)}, u32[]{:S(2)}) collective-permute-start(bf16[2,16,1024]{2,1,0:T(8,128)(2,1)} %get-tuple-element.46), channel_id=1, source_target_pairs={{0,6},{1,7},{2,4},{3,5},{4,2},{5,3},{6,0},{7,1},{8,14},{9,15},{10,... | collective-permute-start | bytes 196616 | tf_op jit(solution)/shard_map/ppermute | solution.py:264
  48.2 3.8 %copy-start.25 = (f32[4,1024]{1,0:T(4,128)}, f32[4,1024]{1,0:T(4,128)S(1)}, u32[]{:S(2)}) copy-start(f32[4,1024]{1,0:T(4,128)S(1)} %collective-permute-done.2.refs_2_) | copy-start | bytes 49156
  48.2 12.9 %collective-permute-start.22 = (bf16[2,16,1024]{2,1,0:T(8,128)(2,1)}, bf16[2,16,1024]{2,1,0:T(8,128)(2,1)S(1)}, u32[]{:S(2)}, u32[]{:S(2)}) collective-permute-start(bf16[2,16,1024]{2,1,0:T(8,128)(2,1)} %get-tuple-element.47), channel_id=1, source_target_pairs={{0,8},{1,9},{2,10},{3,11},{4,12},{5,13},{6,14},{7,15},{8,0},{9,1},... | collective-permute-start | bytes 196616 | tf_op jit(solution)/shard_map/ppermute | solution.py:264
  49.4 0.7 copy-start.1
  49.4 3.8 %collective-permute-start.1 = (f32[4,1024]{1,0:T(4,128)S(1)}, f32[4,1024]{1,0:T(4,128)S(1)}, u32[]{:S(2)}, u32[]{:S(2)}) collective-permute-start(f32[4,1024]{1,0:T(4,128)S(1)} %pad_maximum_fusion.refs_0_), channel_id=1, source_target_pairs={{0,2},{1,3},{2,0},{3,1},{4,6},{5,7},{6,4},{7,5},{8,10},{9,11},{10,... | collective-permute-start | bytes 49160 | tf_op jit(solution)/shard_map/ppermute | solution.py:264
  50.2 3.1 %copy-start.31 = (bf16[2,16,1024]{2,1,0:T(8,128)(2,1)S(1)}, bf16[2,16,1024]{2,1,0:T(8,128)(2,1)}, u32[]{:S(2)}) copy-start(bf16[2,16,1024]{2,1,0:T(8,128)(2,1)} %get-tuple-element.48) | copy-start | bytes 196612
  50.2 5.6 %copy-start.30 = (bf16[2,16,1024]{2,1,0:T(8,128)(2,1)S(1)}, bf16[2,16,1024]{2,1,0:T(8,128)(2,1)}, u32[]{:S(2)}) copy-start(bf16[2,16,1024]{2,1,0:T(8,128)(2,1)} %get-tuple-element.49) | copy-start | bytes 196612
  50.2 6.5 %copy-start.29 = (bf16[2,16,1024]{2,1,0:T(8,128)(2,1)S(1)}, bf16[2,16,1024]{2,1,0:T(8,128)(2,1)}, u32[]{:S(2)}) copy-start(bf16[2,16,1024]{2,1,0:T(8,128)(2,1)} %get-tuple-element.50) | copy-start | bytes 196612
  53.2 19.3 %copy-start.26 = (f32[4,1024]{1,0:T(4,128)}, f32[4,1024]{1,0:T(4,128)S(1)}, u32[]{:S(2)}) copy-start(f32[4,1024]{1,0:T(4,128)S(1)} %collective-permute-done.1.refs_1_) | copy-start | bytes 49156
  53.3 7.9 %collective-permute-start.23 = (bf16[2,16,1024]{2,1,0:T(8,128)(2,1)S(1)}, bf16[2,16,1024]{2,1,0:T(8,128)(2,1)S(1)}, u32[]{:S(2)}, u32[]{:S(2)}) collective-permute-start(bf16[2,16,1024]{2,1,0:T(8,128)(2,1)S(1)} %copy-done.31), channel_id=1, source_target_pairs={{0,10},{1,11},{2,8},{3,9},{4,14},{5,15},{6,12},{7,13},{8,2},{9,3},... | collective-permute-start | bytes 196616 | tf_op jit(solution)/shard_map/ppermute | solution.py:264
  55.7 19.9 %copy-start.5 = (bf16[2,16,1024]{2,1,0:T(8,128)(2,1)}, bf16[2,16,1024]{2,1,0:T(8,128)(2,1)S(1)}, u32[]{:S(2)}) copy-start(bf16[2,16,1024]{2,1,0:T(8,128)(2,1)S(1)} %collective-permute-done.19.refs_11_) | copy-start | bytes 196612
  55.7 7.6 %collective-permute-start.24 = (bf16[2,16,1024]{2,1,0:T(8,128)(2,1)S(1)}, bf16[2,16,1024]{2,1,0:T(8,128)(2,1)S(1)}, u32[]{:S(2)}, u32[]{:S(2)}) collective-permute-start(bf16[2,16,1024]{2,1,0:T(8,128)(2,1)S(1)} %copy-done.30), channel_id=1, source_target_pairs={{0,12},{1,13},{2,14},{3,15},{4,8},{5,9},{6,10},{7,11},{8,4},{9,5},... | collective-permute-start | bytes 196616 | tf_op jit(solution)/shard_map/ppermute | solution.py:264
  56.7 18.9 %copy-start.6 = (bf16[2,16,1024]{2,1,0:T(8,128)(2,1)}, bf16[2,16,1024]{2,1,0:T(8,128)(2,1)S(1)}, u32[]{:S(2)}) copy-start(bf16[2,16,1024]{2,1,0:T(8,128)(2,1)S(1)} %collective-permute-done.20.refs_12_) | copy-start | bytes 196612
  56.7 7.5 %collective-permute-start.25 = (bf16[2,16,1024]{2,1,0:T(8,128)(2,1)S(1)}, bf16[2,16,1024]{2,1,0:T(8,128)(2,1)S(1)}, u32[]{:S(2)}, u32[]{:S(2)}) collective-permute-start(bf16[2,16,1024]{2,1,0:T(8,128)(2,1)S(1)} %copy-done.29), channel_id=1, source_target_pairs={{0,14},{1,15},{2,12},{3,13},{4,10},{5,11},{6,8},{7,9},{8,6},{9,7},... | collective-permute-start | bytes 196616 | tf_op jit(solution)/shard_map/ppermute | solution.py:264
  59.8 15.9 %copy-start.7 = (bf16[2,16,1024]{2,1,0:T(8,128)(2,1)}, bf16[2,16,1024]{2,1,0:T(8,128)(2,1)S(1)}, u32[]{:S(2)}) copy-start(bf16[2,16,1024]{2,1,0:T(8,128)(2,1)S(1)} %collective-permute-done.21.refs_13_) | copy-start | bytes 196612
  59.8 7.2 %collective-permute-start.10 = (bf16[2,16,1024]{2,1,0:T(8,128)(2,1)}, bf16[2,16,1024]{2,1,0:T(8,128)(2,1)S(1)}, u32[]{:S(2)}, u32[]{:S(2)}) collective-permute-start(bf16[2,16,1024]{2,1,0:T(8,128)(2,1)} %get-tuple-element.35), channel_id=1, source_target_pairs={{0,2},{1,3},{2,0},{3,1},{4,6},{5,7},{6,4},{7,5},{8,10},{9,11},{10,... | collective-permute-start | bytes 196616 | tf_op jit(solution)/shard_map/ppermute | solution.py:264
  61.2 14.6 %copy-start.8 = (bf16[2,16,1024]{2,1,0:T(8,128)(2,1)}, bf16[2,16,1024]{2,1,0:T(8,128)(2,1)S(1)}, u32[]{:S(2)}) copy-start(bf16[2,16,1024]{2,1,0:T(8,128)(2,1)S(1)} %collective-permute-done.22.refs_14_) | copy-start | bytes 196612
  61.2 6.8 %collective-permute-start.11 = (bf16[2,16,1024]{2,1,0:T(8,128)(2,1)}, bf16[2,16,1024]{2,1,0:T(8,128)(2,1)S(1)}, u32[]{:S(2)}, u32[]{:S(2)}) collective-permute-start(bf16[2,16,1024]{2,1,0:T(8,128)(2,1)} %get-tuple-element.36), channel_id=1, source_target_pairs={{0,4},{1,5},{2,6},{3,7},{4,0},{5,1},{6,2},{7,3},{8,12},{9,13},{10,... | collective-permute-start | bytes 196616 | tf_op jit(solution)/shard_map/ppermute | solution.py:264
  61.2 14.5 %copy-start.9 = (bf16[2,16,1024]{2,1,0:T(8,128)(2,1)}, bf16[2,16,1024]{2,1,0:T(8,128)(2,1)S(1)}, u32[]{:S(2)}) copy-start(bf16[2,16,1024]{2,1,0:T(8,128)(2,1)S(1)} %collective-permute-done.23.refs_15_) | copy-start | bytes 196612
  61.2 14.4 %collective-permute-start.12 = (bf16[2,16,1024]{2,1,0:T(8,128)(2,1)}, bf16[2,16,1024]{2,1,0:T(8,128)(2,1)S(1)}, u32[]{:S(2)}, u32[]{:S(2)}) collective-permute-start(bf16[2,16,1024]{2,1,0:T(8,128)(2,1)} %get-tuple-element.37), channel_id=1, source_target_pairs={{0,6},{1,7},{2,4},{3,5},{4,2},{5,3},{6,0},{7,1},{8,14},{9,15},{10,... | collective-permute-start | bytes 196616 | tf_op jit(solution)/shard_map/ppermute | solution.py:264
  63.3 12.4 %copy-start.10 = (bf16[2,16,1024]{2,1,0:T(8,128)(2,1)}, bf16[2,16,1024]{2,1,0:T(8,128)(2,1)S(1)}, u32[]{:S(2)}) copy-start(bf16[2,16,1024]{2,1,0:T(8,128)(2,1)S(1)} %collective-permute-done.24.refs_16_) | copy-start | bytes 196612
  63.3 12.3 %collective-permute-start.13 = (bf16[2,16,1024]{2,1,0:T(8,128)(2,1)}, bf16[2,16,1024]{2,1,0:T(8,128)(2,1)S(1)}, u32[]{:S(2)}, u32[]{:S(2)}) collective-permute-start(bf16[2,16,1024]{2,1,0:T(8,128)(2,1)} %get-tuple-element.38), channel_id=1, source_target_pairs={{0,8},{1,9},{2,10},{3,11},{4,12},{5,13},{6,14},{7,15},{8,0},{9,1},... | collective-permute-start | bytes 196616 | tf_op jit(solution)/shard_map/ppermute | solution.py:264
  64.2 11.5 %copy-start.11 = (bf16[2,16,1024]{2,1,0:T(8,128)(2,1)}, bf16[2,16,1024]{2,1,0:T(8,128)(2,1)S(1)}, u32[]{:S(2)}) copy-start(bf16[2,16,1024]{2,1,0:T(8,128)(2,1)S(1)} %collective-permute-done.25.refs_17_) | copy-start | bytes 196612
  64.2 7.5 %copy-start.28 = (f32[3,128]{1,0:T(4,128)S(1)}, f32[3,128]{1,0:T(4,128)}, u32[]{:S(2)}) copy-start(f32[3,128]{1,0:T(4,128)} %constant.47.clone) | copy-start | bytes 4612
  64.2 11.4 %collective-permute-start.14 = (bf16[2,16,1024]{2,1,0:T(8,128)(2,1)}, bf16[2,16,1024]{2,1,0:T(8,128)(2,1)S(1)}, u32[]{:S(2)}, u32[]{:S(2)}) collective-permute-start(bf16[2,16,1024]{2,1,0:T(8,128)(2,1)} %get-tuple-element.39), channel_id=1, source_target_pairs={{0,10},{1,11},{2,8},{3,9},{4,14},{5,15},{6,12},{7,13},{8,2},{9,3},... | collective-permute-start | bytes 196616 | tf_op jit(solution)/shard_map/ppermute | solution.py:264
  67.0 8.7 %copy-start.12 = (bf16[2,16,1024]{2,1,0:T(8,128)(2,1)}, bf16[2,16,1024]{2,1,0:T(8,128)(2,1)S(1)}, u32[]{:S(2)}) copy-start(bf16[2,16,1024]{2,1,0:T(8,128)(2,1)S(1)} %collective-permute-done.10.refs_2_) | copy-start | bytes 196612
  67.0 8.6 %collective-permute-start.15 = (bf16[2,16,1024]{2,1,0:T(8,128)(2,1)}, bf16[2,16,1024]{2,1,0:T(8,128)(2,1)S(1)}, u32[]{:S(2)}, u32[]{:S(2)}) collective-permute-start(bf16[2,16,1024]{2,1,0:T(8,128)(2,1)} %get-tuple-element.40), channel_id=1, source_target_pairs={{0,12},{1,13},{2,14},{3,15},{4,8},{5,9},{6,10},{7,11},{8,4},{9,5},... | collective-permute-start | bytes 196616 | tf_op jit(solution)/shard_map/ppermute | solution.py:264
  68.0 7.8 %copy-start.13 = (bf16[2,16,1024]{2,1,0:T(8,128)(2,1)}, bf16[2,16,1024]{2,1,0:T(8,128)(2,1)S(1)}, u32[]{:S(2)}) copy-start(bf16[2,16,1024]{2,1,0:T(8,128)(2,1)S(1)} %collective-permute-done.11.refs_3_) | copy-start | bytes 196612
  68.0 7.7 %collective-permute-start.16 = (bf16[2,16,1024]{2,1,0:T(8,128)(2,1)}, bf16[2,16,1024]{2,1,0:T(8,128)(2,1)S(1)}, u32[]{:S(2)}, u32[]{:S(2)}) collective-permute-start(bf16[2,16,1024]{2,1,0:T(8,128)(2,1)} %get-tuple-element.41), channel_id=1, source_target_pairs={{0,14},{1,15},{2,12},{3,13},{4,10},{5,11},{6,8},{7,9},{8,6},{9,7},... | collective-permute-start | bytes 196616 | tf_op jit(solution)/shard_map/ppermute | solution.py:264
  75.6 0.6 copy-start.14
  75.6 0.6 copy-start.15
  75.6 0.6 copy-start.16
  75.7 0.7 copy-start.17
  75.7 0.7 copy-start.18
where the time goes:
time: 91.7 us; the launch traced here: 91.4 us
  starting transfers between devices  41 us (45%)
  Pallas kernels  31.7 us (35%)
  waiting for transfers between devices  12 us (13%)
  local copies, waits for them, and re-layouts  5.17 us (6%)
  other arithmetic  1.25 us (1%)
    ppermute x21, starting transfers between devices, between(): return lax.ppermute(x, 'space', [(i, i ^ 2 * k) for i in range(devices)])  31.8 us
    pallas_call x1, Pallas kernels, sweeps(): pl.pallas_call(sweep_kernel, out_shape=jax.ShapeDtypeStruct((rows, 2 * pa...  15.1 us
    pallas_call x2, Pallas kernels, transform(): pl.pallas_call(functools.partial(transform_kernel, outer), out_shape=(sha...  9.91 us
    ppermute x1, waiting for transfers between devices, on_device(): lax.ppermute(lax.dynamic_slice_in_dim(field, core, 1, 0), 'space', across)  5.7 us
    ppermute x1, starting transfers between devices, on_device(): lax.ppermute(lax.dynamic_slice_in_dim(field, core, 1, 0), 'space', across)  5.54 us
    ppermute x21, waiting for transfers between devices, between(): return lax.ppermute(x, 'space', [(i, i ^ 2 * k) for i in range(devices)])  5.08 us
    pallas_call x2, Pallas kernels, assemble(): pl.pallas_call(assemble_kernel, out_shape=[jax.ShapeDtypeStruct((2, share...  3.63 us
    ppermute x2, starting transfers between devices, on_device(): other = lax.ppermute(other, 'space', partner)  3.18 us
  transfers between devices with their start and end apart: 26, of which 6 were waited for; matrix products, arithmetic and copies ran while one was open for 2% of the time, Pallas kernels for 18%

commit v1 on v0

v1 whole, which is shorter than its diff:
```python
import functools
import math

import jax
import jax.numpy as jnp
import numpy as np
from jax import lax
from jax.experimental import pallas as pl
from jax.experimental.pallas import tpu as pltpu
from jax.sharding import PartitionSpec as P

SWEEPS = 4
VMEM = pl.BlockSpec(memory_space=pltpu.VMEM)
SMEM = pl.BlockSpec(memory_space=pltpu.SMEM)


def slot_order(steps, devices):
    share = steps // devices
    order = []
    for core in range(2):
        for chip in range(devices // 2):
            first = (chip * 2 + core) * share
            order += list(range(first, first + share, 2)) + list(range(first + 1, first + share, 2))
    return np.array(order)


def transform_tables(steps, devices):
    index = np.arange(steps)
    freqs = np.where(index == 1, steps // 2, index // 2)
    use_cos = (index % 2 == 0) | (index == 1)
    phase = 2.0 * np.pi / steps * (freqs[:, None] * index[None, :] % steps)
    table = np.where(use_cos[:, None], np.cos(phase), -np.sin(phase)) / math.sqrt(steps)
    table = table[slot_order(steps, devices)]
    high = table.astype(jnp.bfloat16)
    low = (table - high.astype(np.float64)).astype(jnp.bfloat16)
    return high, low


def symbol_tables(steps):
    pair = np.arange(steps // 2)

    def real_part(freq):
        theta = 2.0 * np.pi / steps * freq
        return 11.0 / 6.0 - 3.0 * np.cos(theta) + 1.5 * np.cos(2.0 * theta) - np.cos(3.0 * theta) / 3.0

    theta = 2.0 * np.pi / steps * pair
    cross = 3.0 * np.sin(theta) - 1.5 * np.sin(2.0 * theta) + np.sin(3.0 * theta) / 3.0
    second = np.where(pair == 0, steps // 2, pair)
    return np.stack([real_part(pair), real_part(second), cross]).astype(np.float32)


def transform_kernel(outer, scal, field, halo, hist, source, row_c, col_c, high, low, own, other, *refs):
    *spare, r_high, r_low = refs
    core, chip = scal[0], scal[1]
    row = core if outer else 1 - core
    beside = 1 - row
    steps, cols = r_high.shape
    rc = 0.5 * row_c[...]
    cc = 0.5 * col_c[pl.ds(row, 1)]
    cl = pltpu.roll(cc, 1, 1)
    diag = 2.0 * rc + cc + cl
    tile = 16
    if spare:
        spare[0][0] = field[beside]

    def at(i, before):
        rows = pl.ds(pl.multiple_of(i * tile, tile), tile)
        c = field[row, rows, :].astype(jnp.float32)
        near = field[beside, rows, :].astype(jnp.float32) + halo[0, rows, :].astype(jnp.float32)
        seq = jnp.concatenate([before, c], axis=0)
        back = (
            11.0 / 6.0 * c
            - 3.0 * seq[7 : 7 + tile]
            + 1.5 * seq[6 : 6 + tile]
            - seq[5 : 5 + tile] / 3.0
        )
        flux = diag * c - rc * near - cc * pltpu.roll(c, cols - 1, 1) - cl * pltpu.roll(c, 1, 1)
        res = source[row, rows, :].astype(jnp.float32) - back - flux
        upper = res.astype(jnp.bfloat16)
        r_high[rows, :] = upper
        r_low[rows, :] = (res - upper.astype(jnp.float32)).astype(jnp.bfloat16)
        return c[tile - 8 :]

    lax.fori_loop(0, steps // tile, at, hist[row])
    half = steps // 2
    chips, share, _ = own.shape
    width = min(cols, 256)
    for ref, which in ((other, 1 - core), (own, core)):
        part = pl.ds(pl.multiple_of(which * half, half), half)
        for j in range(0, cols, width):
            a, b = r_high[:, j : j + width], r_low[:, j : j + width]
            acc = jnp.dot(high[part, :], a, preferred_element_type=jnp.float32)
            acc += jnp.dot(high[part, :], b, preferred_element_type=jnp.float32)
            acc += jnp.dot(low[part, :], a, preferred_element_type=jnp.float32)
            acc = acc.astype(jnp.bfloat16)
            for g in range(chips):
                ref[g ^ chip, :, j : j + width] = acc[g * share : (g + 1) * share]


def transform(outer, scal, field, halo, hist, source, row_c, col_c, tables, devices):
    _, steps, cols = field.shape
    shape = jax.ShapeDtypeStruct((devices // 2, steps // devices, cols), jnp.bfloat16)
    spare = [] if outer else [jax.ShapeDtypeStruct((1, steps, cols), jnp.bfloat16)]
    return pl.pallas_call(
        functools.partial(transform_kernel, outer),
        out_shape=[shape, shape] + spare,
        in_specs=[SMEM] + [VMEM] * 8,
        out_specs=[VMEM] * (2 + len(spare)),
        scratch_shapes=[pltpu.VMEM((steps, cols), jnp.bfloat16)] * 2,
        cost_estimate=pl.CostEstimate(
            flops=6 * steps * steps * cols, bytes_accessed=4 * steps * cols * 2, transcendentals=0
        ),
        compiler_params=pltpu.CompilerParams(vmem_limit_bytes=8 * 2**20),
        name="transform",
    )(scal, field, halo, hist, source, row_c, col_c, *tables)


def put_face(face, out, first):
    high = face[...].astype(jnp.bfloat16)
    low = (face[...] - high.astype(jnp.float32)).astype(jnp.bfloat16)
    out[first : first + 8, :] = jnp.concatenate([high, low], axis=0)


def get_face(pack, first):
    both = pack[first : first + 8, :].astype(jnp.float32)
    return both[:4] + both[4:]


def assemble_kernel(phases, face, *refs):
    ins, outs = refs[: 2 * phases], refs[2 * phases :]
    chips, share, _ = ins[0].shape
    far, near = outs[: chips // 2], outs[chips // 2 :]
    for n, out in enumerate(far):
        for side in range(2):
            out[side * share : (side + 1) * share, :] = ins[2 * phases - 2 + side][chips // 2 + n]
        if phases == 1:
            put_face(face, out, 2 * share)
    for n, out in enumerate(near):
        for side in range(2 * phases):
            out[side * share : (side + 1) * share, :] = ins[side][1 + n]
        put_face(face, out, 2 * phases * share)


def assemble(face, parts):
    chips, share, cols = parts[0].shape
    phases = len(parts) // 2
    far = jax.ShapeDtypeStruct((2 * share + (8 if phases == 1 else 0), cols), jnp.bfloat16)
    near = jax.ShapeDtypeStruct((4 * share + 8, cols), jnp.bfloat16)
    shapes = [far] * (chips // 2) + ([near] * (chips // 2 - 1) if phases == 2 else [])
    return pl.pallas_call(
        functools.partial(assemble_kernel, phases),
        out_shape=shapes,
        in_specs=[VMEM] * (1 + len(parts)),
        out_specs=[VMEM] * len(shapes),
        cost_estimate=pl.CostEstimate(
            flops=0, bytes_accessed=4 * chips * share * cols * 2, transcendentals=0
        ),
        compiler_params=pltpu.CompilerParams(vmem_limit_bytes=4 * 2**20),
        name="assemble",
    )(face, *parts)


def coefficient_kernel(ks, first_row, scal, row_c, symbols, *refs):
    packs, outs = refs[: len(ks)], refs[-5:]
    first, second, cross, ahead, behind = outs
    core, chip = scal[0], scal[1]
    rc = 0.5 * row_c[...]
    inverse_rc = 1.0 / rc
    one, two, skew = symbols[0], symbols[1], symbols[2]
    for k, pack in zip(ks, packs):
        face = 0.5 * (pack[...] if k == 0 else get_face(pack, first_row))
        for j in range(4):
            side = core if j < 2 else 1 - core
            at = (chip ^ k) * 4 + side * 2 + j % 2
            cc = face[j : j + 1, :]
            cl = pltpu.roll(cc, 1, 1)
            diag = 2.0 * rc + cc + cl
            p0 = one + diag
            p1 = two + diag
            inverse = rc / (p0 * p1 + skew * skew)
            first[at] = p1 * inverse
            second[at] = p0 * inverse
            cross[at] = skew * inverse
            ahead[at] = cc * inverse_rc
            behind[at] = cl * inverse_rc


def coefficients(scal, row_c, symbols, ks, packs, first_row, before, chips):
    rows = 4 * chips
    pairs = symbols.shape[1]
    cols = row_c.shape[1]
    big = jax.ShapeDtypeStruct((rows, pairs, cols), jnp.float32)
    thin = jax.ShapeDtypeStruct((rows, 1, cols), jnp.float32)
    count = 3 + len(ks)
    return pl.pallas_call(
        functools.partial(coefficient_kernel, ks, first_row),
        out_shape=[big, big, big, thin, thin],
        in_specs=[SMEM] + [VMEM] * (2 + len(ks)) + [pl.BlockSpec(memory_space=pl.ANY)] * len(before),
        out_specs=[VMEM] * 5,
        input_output_aliases={count + n: n for n in range(len(before))},
        cost_estimate=pl.CostEstimate(
            flops=40 * len(ks) * pairs * cols,
            bytes_accessed=48 * len(ks) * pairs * cols,
            transcendentals=0,
        ),
        compiler_params=pltpu.CompilerParams(vmem_limit_bytes=8 * 2**20),
        name="coefficients",
    )(scal, row_c, symbols, *packs, *before)


def sweep_kernel(scal, row_c, first, second, cross, ahead, behind, *refs):
    *blocks, out, w_re, w_im, a_re, a_im, b_re, b_im, mixed = refs
    core, chip = scal[0], scal[1]
    rows, pairs, cols = w_re.shape
    chips = rows // 4
    share = 2 * pairs
    group = math.gcd(rows, 8)
    scale = 2.0 / row_c[...]

    def solve(i, t0, t1):
        s = cross[i]
        return first[i] * t0 + s * t1, second[i] * t1 - s * t0

    def enter(block, k, side, outer):
        owner = core if side == 0 else 1 - core
        row = owner if outer else 1 - owner
        i = (chip ^ k) * 4 + owner * 2 + row
        both = block.astype(jnp.float32)
        w_re[i], w_im[i] = solve(i, scale * both[:pairs], scale * both[pairs:])

    own_in, other_in, own_out, other_out = blocks[:4]
    far_in = blocks[4 : 4 + chips // 2]
    far_out = blocks[4 + chips // 2 : 4 + chips]
    near = blocks[4 + chips :]
    for side, block in enumerate((own_in, other_in, own_out, other_out)):
        enter(block[0], 0, side % 2, side >= 2)
    for outer, packs in ((False, far_in), (True, far_out)):
        for n, pack in enumerate(packs):
            for side in range(2):
                enter(pack[side * share : (side + 1) * share, :], chips // 2 + n, side, outer)
    for n, pack in enumerate(near):
        for side in range(4):
            enter(pack[side * share : (side + 1) * share, :], 1 + n, side % 2, side >= 2)

    def sweep(src, dst):
        def at(q, carry):
            i0 = q * group
            lines = [jnp.where(i0 == 0, rows - 1, i0 - 1)]
            lines += [i0 + n for n in range(group)]
            lines += [jnp.where(i0 + group == rows, 0, i0 + group)]
            for up, i, down in zip(lines, lines[1:], lines[2:]):
                u = []
                for z in src:
                    c = z[i]
                    u.append(
                        (z[up] + z[down])
                        + ahead[i] * pltpu.roll(c, cols - 1, 1)
                        + behind[i] * pltpu.roll(c, 1, 1)
                    )
                z0, z1 = solve(i, *u)
                z0, z1 = w_re[i] + z0, w_im[i] + z1
                if dst is not None:
                    dst[0][i], dst[1][i] = z0, z1
                    continue
                for j in range(mixed.shape[0]):
                    lanes = slice(j * 128, (j + 1) * 128)
                    mixed[j, pl.ds(0, pairs, stride=2), :] = z0[:, lanes]
                    mixed[j, pl.ds(1, pairs, stride=2), :] = z1[:, lanes]
                    out[i, :, lanes] = mixed[j].astype(out.dtype)
            return carry

        lax.fori_loop(0, rows // group, at, 0)

    src = (w_re, w_im)
    spaces = ((a_re, a_im), (b_re, b_im))
    for step in range(SWEEPS - 1):
        dst = None if step == SWEEPS - 2 else spaces[step % 2]
        sweep(src, dst)
        src = dst


def sweeps(scal, row_c, coeffs, blocks):
    rows, pairs, cols = coeffs[0].shape
    return pl.pallas_call(
        sweep_kernel,
        out_shape=jax.ShapeDtypeStruct((rows, 2 * pairs, cols), jnp.bfloat16),
        in_specs=[SMEM] + [VMEM] * (6 + len(blocks)),
        out_specs=VMEM,
        scratch_shapes=[pltpu.VMEM((rows, pairs, cols), jnp.float32)] * 6
        + [pltpu.VMEM((cols // 128, 2 * pairs, 128), jnp.float32)],
        cost_estimate=pl.CostEstimate(
            flops=80 * rows * pairs * cols, bytes_accessed=60 * rows * pairs * cols, transcendentals=0
        ),
        compiler_params=pltpu.CompilerParams(vmem_limit_bytes=16 * 2**20),
        name="sweeps",
    )(scal, row_c, *coeffs, *blocks)


def on_device(field, history, source, row_conduct, col_conduct):
    devices = lax.axis_size("space")
    chips = devices // 2
    steps, cols = field.shape[1:]
    share = steps // devices
    me = lax.axis_index("space")
    core, chip = me % 2, me // 2
    scal = jnp.stack([core, chip]).astype(jnp.int32)
    row_c = row_conduct.reshape(1, cols)
    partner = [(i, i ^ 1) for i in range(devices)]
    across = [(i, (i - 1 if i % 2 == 0 else i + 1) % devices) for i in range(devices)]
    tables = transform_tables(steps, devices)
    earlier = jnp.pad(
        jnp.transpose(history, (1, 0, 2)).astype(jnp.float32), ((0, 0), (5, 0), (0, 0))
    )
    args = (earlier, source, row_c, col_conduct, tables, devices)

    def send(x, pairs):
        return lax.ppermute(x, "space", pairs)

    def between(pack, k):
        return send(pack, [(i, i ^ (2 * k)) for i in range(devices)])

    halo = send(lax.dynamic_slice_in_dim(field, 1 - core, 1, 0), partner)
    face = jnp.concatenate([col_conduct, send(col_conduct, partner)], axis=0)
    own_in, other_in, spare = transform(False, scal, field, halo, *args)
    other_in = send(other_in, partner)
    halo = send(spare, across)
    packs = assemble(face, (own_in, other_in))
    far = range(chips // 2, chips)
    near = range(1, chips // 2)
    far_in = [between(pack, k) for pack, k in zip(packs, far)]
    own_out, other_out = transform(True, scal, field, halo, *args)
    other_out = send(other_out, partner)
    packs = assemble(face, (own_in, other_in, own_out, other_out))
    far_out = [between(pack, k) for pack, k in zip(packs, far)]
    near_all = [between(pack, k) for pack, k in zip(packs[chips // 2 :], near)]

    pairs = share // 2
    symbols = lax.dynamic_slice_in_dim(jnp.asarray(symbol_tables(steps)), me * pairs, pairs, 1)
    symbols = symbols[:, :, None]
    coeffs = coefficients(scal, row_c, symbols, (0, *far), (face, *far_in), 2 * share, (), chips)
    coeffs = coefficients(
        scal, row_c, symbols, tuple(near), near_all, 4 * share, coeffs, chips
    )
    blocks = (own_in, other_in, own_out, other_out, *far_in, *far_out, *near_all)
    return sweeps(scal, row_c, coeffs, blocks)


def solution(mesh):
    in_specs = (
        P(("groups", "space"), None, None),
        P(None, ("groups", "space"), None),
        P(("groups", "space"), None, None),
        P("groups"),
        P(("groups", "space"), None),
    )
    out_specs = P("groups", "space", None)

    return jax.shard_map(
        on_device, mesh=mesh, in_specs=in_specs, out_specs=out_specs, check_vma=False
    )
```

time: 91.7 us -> 65.7 us (0.72)
  Pallas kernels: 31.7 us -> 14.5 us
  starting transfers between devices: 41 us -> 31.2 us
  waiting for transfers between devices: 12 us -> 16 us
  local copies, waits for them, and re-layouts: 5.17 us -> 3.5 us
  other arithmetic: 1.25 us -> 0.1 us
    ppermute x26 -> x16, starting transfers between devices: 41 us -> 31.2 us  [send(): return lax.ppermute(x, 'space', pairs)]
    pallas_call x5 -> x6, Pallas kernels: 16.6 us -> 7.93 us  [the longest x2 5.99 us: transform(): pl.pallas_call(functools.partial(transform_kernel, outer), out_shape=[sha...]
    pallas_call x1, Pallas kernels: 15.1 us -> 6.54 us  [sweeps(): pl.pallas_call(sweep_kernel, out_shape=jax.ShapeDtypeStruct((rows, 2 * pa...]
    ppermute x26 -> x16, waiting for transfers between devices: 12 us -> 16 us  [send(): return lax.ppermute(x, 'space', pairs)]
    unnamed x65 -> x17, local copies, waits for them, and re-layouts: 3.14 us -> 2.16 us
  transfers between devices with their start and end apart: 26 -> 16, of which waited for: 6 -> 5; matrix products, arithmetic and copies ran while one was open for 2% -> 0% of each run, Pallas kernels for 18% -> 8%
where the time goes in v1:
time: 65.7 us; the launch traced here: 65.5 us
  starting transfers between devices  31.2 us (47%)
  waiting for transfers between devices  16 us (24%)
  Pallas kernels  14.5 us (22%)
  local copies, waits for them, and re-layouts  3.5 us (5%)
    ppermute x16, starting transfers between devices, send(): return lax.ppermute(x, 'space', pairs)  31.2 us
    ppermute x16, waiting for transfers between devices, send(): return lax.ppermute(x, 'space', pairs)  16 us
    pallas_call x1, Pallas kernels, sweeps(): pl.pallas_call(sweep_kernel, out_shape=jax.ShapeDtypeStruct((rows, 2 * pa...  6.54 us
    pallas_call x2, Pallas kernels, transform(): pl.pallas_call(functools.partial(transform_kernel, outer), out_shape=[sha...  5.99 us
    unnamed x17, local copies, waits for them, and re-layouts  2.16 us
    pallas_call x2, Pallas kernels, coefficients(): pl.pallas_call(functools.partial(coefficient_kernel, ks, first_row), out_...  1.87 us
  transfers between devices with their start and end apart: 16, of which 5 were waited for; matrix products, arithmetic and copies ran while one was open for 0% of the time, Pallas kernels for 8%

profile of v1, /device:TPU:0, one launch (start us, length us, event | category | flops | bytes accessed | tf_op | source)
XLA Modules:
  0.0 65.5 jit_solution(10894867918071085450)
XLA Ops:
  0.0 0.0 copy-start
  0.0 0.0 copy-start.6
  0.0 0.0 copy-start.5
  0.0 1.2 %constant_dynamic-slice_fusion = bf16[1,256,1024]{2,1,0:T(8,128)(2,1)S(1)} fusion(bf16[2,256,1024]{2,1,0:T(8,128)(2,1)} %field.3, s32[]{:T(128)S(6)} %select_n.20), kind=kLoop, calls=%fused_computation.5 | loop fusion | bytes 1048580 | tf_op jit(solution)/shard_map/dynamic_slice | solution.py:322
  1.2 0.0 copy-start.2
  1.2 0.6 collective-permute-start.1
  1.8 0.0 copy-done.6
  1.8 0.1 pad_add_fusion.scal
  1.9 0.0 copy-start.4
  1.9 1.4 %collective-permute-done.1.halo = bf16[1,256,1024]{2,1,0:T(8,128)(2,1)S(1)} collective-permute-done((bf16[1,256,1024]{2,1,0:T(8,128)(2,1)S(1)}, bf16[1,256,1024]{2,1,0:T(8,128)(2,1)S(1)}, u32[]{:S(2)}, u32[]{:S(2)}) %collective-permute-start.1) | collective-permute-done | bytes 524320 | tf_op jit(solution)/shard_map/ppermute | solution.py:317
  3.3 0.0 copy-done
  3.3 0.0 copy-done.5
  3.3 0.0 copy-done.2
  3.3 0.0 copy-done.4
  3.3 0.0 copy-start.1
  3.3 1.2 %copy-done.1 = bf16[2,256,1024]{2,1,0:T(8,128)(2,1)S(1)} copy-done((bf16[2,256,1024]{2,1,0:T(8,128)(2,1)S(1)}, bf16[2,256,1024]{2,1,0:T(8,128)(2,1)}, u32[]{:S(2)}) %copy-start.1) | copy-done | bytes 1048600
  4.5 0.0 copy-start.3
  4.5 0.9 %copy-done.3 = bf16[256,256]{1,0:T(8,128)(2,1)S(1)} copy-done((bf16[256,256]{1,0:T(8,128)(2,1)S(1)}, bf16[256,256]{1,0:T(8,128)(2,1)}, u32[]{:S(2)}) %copy-start.3) | copy-done | bytes 131096
  5.4 3.0 %transform.2 = (bf16[8,16,1024]{2,1,0:T(8,128)(2,1)S(1)}, bf16[8,16,1024]{2,1,0:T(8,128)(2,1)S(1)}, bf16[1,256,1024]{2,1,0:T(8,128)(2,1)S(1)}) custom-call(s32[2]{0:T(128)S(1)} %pad_add_fusion.scal, bf16[2,256,1024]{2,1,0:T(8,128)(2,1)S(1)} %copy-done, bf16[1,256,1024]{2,1,0:T(8,128)(2,1)S(1)} %collective-permute-done.1.halo, ...), custom_call_target="tpu_custom_call" | custom-call | flops 402653184 | bytes 2097152 | tf_op jit(solution)/shard_map/transform/pallas_call | solution.py:104
  8.4 5.7 %collective-permute-start.3 = (bf16[1,256,1024]{2,1,0:T(8,128)(2,1)S(1)}, bf16[1,256,1024]{2,1,0:T(8,128)(2,1)S(1)}, u32[]{:S(2)}, u32[]{:S(2)}) collective-permute-start(bf16[1,256,1024]{2,1,0:T(8,128)(2,1)S(1)} %get-tuple-element.33), channel_id=1, source_target_pairs={{0,15},{1,2},{2,1},{3,4},{4,3},{5,6},{6,5},{7,8},{8,7},{9,10},{10,... | collective-permute-start | bytes 1572872 | tf_op jit(solution)/shard_map/ppermute | solution.py:317
  14.2 0.0 collective-permute-start.2
  14.2 7.0 %collective-permute-done.3.halo = bf16[1,256,1024]{2,1,0:T(8,128)(2,1)S(1)} collective-permute-done((bf16[1,256,1024]{2,1,0:T(8,128)(2,1)S(1)}, bf16[1,256,1024]{2,1,0:T(8,128)(2,1)S(1)}, u32[]{:S(2)}, u32[]{:S(2)}) %collective-permute-start.3) | collective-permute-done | bytes 524320 | tf_op jit(solution)/shard_map/ppermute | solution.py:317
  21.1 3.0 %transform.3 = (bf16[8,16,1024]{2,1,0:T(8,128)(2,1)S(1)}, bf16[8,16,1024]{2,1,0:T(8,128)(2,1)S(1)}) custom-call(s32[2]{0:T(128)S(1)} %pad_add_fusion.scal, bf16[2,256,1024]{2,1,0:T(8,128)(2,1)S(1)} %copy-done, bf16[1,256,1024]{2,1,0:T(8,128)(2,1)S(1)} %collective-permute-done.3.halo, f32[2,8,1024]{2,1,0:T(8,128)S(1)} %pad_convert_fusion.hist, ...), custom_call_target="tpu_custom_call" | custom-call | flops 402653184 | bytes 2097152 | tf_op jit(solution)/shard_map/transform/pallas_call | solution.py:104
  24.1 2.9 %collective-permute-start.4 = (bf16[8,16,1024]{2,1,0:T(8,128)(2,1)S(1)}, bf16[8,16,1024]{2,1,0:T(8,128)(2,1)S(1)}, u32[]{:S(2)}, u32[]{:S(2)}) collective-permute-start(bf16[8,16,1024]{2,1,0:T(8,128)(2,1)S(1)} %get-tuple-element.35), channel_id=1, source_target_pairs={{0,1},{1,0},{2,3},{3,2},{4,5},{5,4},{6,7},{7,6},{8,9},{9,8},{10,11... | collective-permute-start | bytes 786440 | tf_op jit(solution)/shard_map/ppermute | solution.py:317
  27.1 0.1 collective-permute-start
  27.2 1.1 %collective-permute-done = f32[2,1024]{1,0:T(2,128)S(1)} collective-permute-done((f32[2,1024]{1,0:T(2,128)S(1)}, f32[2,1024]{1,0:T(2,128)S(1)}, u32[]{:S(2)}, u32[]{:S(2)}) %collective-permute-start) | collective-permute-done | bytes 8224 | tf_op jit(solution)/shard_map/ppermute | solution.py:317
  28.3 0.0 collective-permute-done.2.refs_1_
  28.3 2.9 %collective-permute-start.8 = (bf16[40,1024]{1,0:T(8,128)(2,1)S(1)}, bf16[40,1024]{1,0:T(8,128)(2,1)S(1)}, u32[]{:S(2)}, u32[]{:S(2)}) collective-permute-start(bf16[40,1024]{1,0:T(8,128)(2,1)S(1)} %get-tuple-element.39), channel_id=1, source_target_pairs={{0,8},{1,9},{2,10},{3,11},{4,12},{5,13},{6,14},{7,15},{8,0},{9,1},... | collective-permute-start | bytes 245768 | tf_op jit(solution)/shard_map/ppermute | solution.py:317
  31.2 0.0 collective-permute-done.4.refs_3_
  31.2 1.8 %collective-permute-start.5 = (bf16[72,1024]{1,0:T(8,128)(2,1)S(1)}, bf16[72,1024]{1,0:T(8,128)(2,1)S(1)}, u32[]{:S(2)}, u32[]{:S(2)}) collective-permute-start(bf16[72,1024]{1,0:T(8,128)(2,1)S(1)} %get-tuple-element.36), channel_id=1, source_target_pairs={{0,2},{1,3},{2,0},{3,1},{4,6},{5,7},{6,4},{7,5},{8,10},{9,11},{10,... | collective-permute-start | bytes 442376 | tf_op jit(solution)/shard_map/ppermute | solution.py:317
  33.1 1.6 %collective-permute-start.6 = (bf16[72,1024]{1,0:T(8,128)(2,1)S(1)}, bf16[72,1024]{1,0:T(8,128)(2,1)S(1)}, u32[]{:S(2)}, u32[]{:S(2)}) collective-permute-start(bf16[72,1024]{1,0:T(8,128)(2,1)S(1)} %get-tuple-element.37), channel_id=1, source_target_pairs={{0,4},{1,5},{2,6},{3,7},{4,0},{5,1},{6,2},{7,3},{8,12},{9,13},{10,... | collective-permute-start | bytes 442376 | tf_op jit(solution)/shard_map/ppermute | solution.py:317
  34.7 0.0 collective-permute-start.9
  34.7 2.5 %collective-permute-start.10 = (bf16[40,1024]{1,0:T(8,128)(2,1)S(1)}, bf16[40,1024]{1,0:T(8,128)(2,1)S(1)}, u32[]{:S(2)}, u32[]{:S(2)}) collective-permute-start(bf16[40,1024]{1,0:T(8,128)(2,1)S(1)} %get-tuple-element.41), channel_id=1, source_target_pairs={{0,12},{1,13},{2,14},{3,15},{4,8},{5,9},{6,10},{7,11},{8,4},{9,5},... | collective-permute-start | bytes 245768 | tf_op jit(solution)/shard_map/ppermute | solution.py:317
  37.2 0.0 collective-permute-done.8.refs_1_.refs_4_
  37.2 3.4 %collective-permute-start.11 = (bf16[40,1024]{1,0:T(8,128)(2,1)S(1)}, bf16[40,1024]{1,0:T(8,128)(2,1)S(1)}, u32[]{:S(2)}, u32[]{:S(2)}) collective-permute-start(bf16[40,1024]{1,0:T(8,128)(2,1)S(1)} %get-tuple-element.42), channel_id=1, source_target_pairs={{0,14},{1,15},{2,12},{3,13},{4,10},{5,11},{6,8},{7,9},{8,6},{9,7},... | collective-permute-start | bytes 245768 | tf_op jit(solution)/shard_map/ppermute | solution.py:317
  40.6 5.7 %collective-permute-done.9.refs_2_.refs_5_ = bf16[40,1024]{1,0:T(8,128)(2,1)S(1)} collective-permute-done((bf16[40,1024]{1,0:T(8,128)(2,1)S(1)}, bf16[40,1024]{1,0:T(8,128)(2,1)S(1)}, u32[]{:S(2)}, u32[]{:S(2)}) %collective-permute-start.9) | collective-permute-done | bytes 81952 | tf_op jit(solution)/shard_map/ppermute | solution.py:317
  46.3 0.0 collective-permute-start.7
  46.3 0.0 collective-permute-done.10.refs_3_.refs_6_
  46.3 1.1 %collective-permute-start.12 = (bf16[32,1024]{1,0:T(8,128)(2,1)S(1)}, bf16[32,1024]{1,0:T(8,128)(2,1)S(1)}, u32[]{:S(2)}, u32[]{:S(2)}) collective-permute-start(bf16[32,1024]{1,0:T(8,128)(2,1)S(1)} %get-tuple-element.53), channel_id=1, source_target_pairs={{0,8},{1,9},{2,10},{3,11},{4,12},{5,13},{6,14},{7,15},{8,0},{9,1},... | collective-permute-start | bytes 196616 | tf_op jit(solution)/shard_map/ppermute | solution.py:317
  47.4 0.0 collective-permute-done.11.refs_4_.refs_7_
  47.4 0.0 copy-start.7
  47.4 3.1 %collective-permute-start.13 = (bf16[32,1024]{1,0:T(8,128)(2,1)S(1)}, bf16[32,1024]{1,0:T(8,128)(2,1)S(1)}, u32[]{:S(2)}, u32[]{:S(2)}) collective-permute-start(bf16[32,1024]{1,0:T(8,128)(2,1)S(1)} %get-tuple-element.54), channel_id=1, source_target_pairs={{0,10},{1,11},{2,8},{3,9},{4,14},{5,15},{6,12},{7,13},{8,2},{9,3},... | collective-permute-start | bytes 196616 | tf_op jit(solution)/shard_map/ppermute | solution.py:317
  50.5 0.0 collective-permute-done.5.refs_0_.refs_12_
  50.5 1.4 %collective-permute-start.14 = (bf16[32,1024]{1,0:T(8,128)(2,1)S(1)}, bf16[32,1024]{1,0:T(8,128)(2,1)S(1)}, u32[]{:S(2)}, u32[]{:S(2)}) collective-permute-start(bf16[32,1024]{1,0:T(8,128)(2,1)S(1)} %get-tuple-element.55), channel_id=1, source_target_pairs={{0,12},{1,13},{2,14},{3,15},{4,8},{5,9},{6,10},{7,11},{8,4},{9,5},... | collective-permute-start | bytes 196616 | tf_op jit(solution)/shard_map/ppermute | solution.py:317
  51.9 0.0 collective-permute-done.6.refs_1_.refs_13_
  51.9 4.1 %collective-permute-start.15 = (bf16[32,1024]{1,0:T(8,128)(2,1)S(1)}, bf16[32,1024]{1,0:T(8,128)(2,1)S(1)}, u32[]{:S(2)}, u32[]{:S(2)}) collective-permute-start(bf16[32,1024]{1,0:T(8,128)(2,1)S(1)} %get-tuple-element.56), channel_id=1, source_target_pairs={{0,14},{1,15},{2,12},{3,13},{4,10},{5,11},{6,8},{7,9},{8,6},{9,7},... | collective-permute-start | bytes 196616 | tf_op jit(solution)/shard_map/ppermute | solution.py:317
  56.0 0.0 copy-done.7
  56.0 0.1 dynamic-slice_bitcast_fusion
  56.1 0.1 copy.16.symbols
  56.2 1.0 %coefficients.2 = (f32[32,8,1024]{2,1,0:T(8,128)S(1)}, f32[32,8,1024]{2,1,0:T(8,128)S(1)}, f32[32,8,1024]{2,1,0:T(8,128)S(1)}, f32[32,1,1024]{2,1,0:T(1,128)S(1)}, f32[32,1,1024]{2,1,0:T(1,128)S(1)}) custom-call(s32[2]{0:T(128)S(1)} %pad_add_fusion.scal, f32[1,1024]{1,0:T(1,128)S(1)} %bitcast.10, f32[3,8,1]{2,1,0:T(8,128)S(1)} %copy.16.symbols, ...), custom_call_target="tpu_custom_call" | custom-call | flops 1638400 | bytes 1966080 | tf_op jit(solution)/shard_map/coefficients/pallas_call | solution.py:195
  57.2 0.0 collective-permute-done.7.refs_2_.refs_14_
  57.2 0.9 %coefficients.3 = (f32[32,8,1024]{2,1,0:T(8,128)S(1)}, f32[32,8,1024]{2,1,0:T(8,128)S(1)}, f32[32,8,1024]{2,1,0:T(8,128)S(1)}, f32[32,1,1024]{2,1,0:T(1,128)S(1)}, f32[32,1,1024]{2,1,0:T(1,128)S(1)}) custom-call(s32[2]{0:T(128)S(1)} %pad_add_fusion.scal, ...), custom_call_target="tpu_custom_call", output_to_operand_aliasing={{0}: (6, {}), {1}: (7, {}), {2}: (8, {}), {3}: (9, {}), {4}... | custom-call | flops 983040 | bytes 1179648 | tf_op jit(solution)/shard_map/coefficients/pallas_call | solution.py:195
  58.1 0.0 collective-permute-done.12.refs_8_
  58.1 0.0 collective-permute-done.13.refs_9_
  58.1 0.0 collective-permute-done.14.refs_10_
  58.1 0.8 %collective-permute-done.15.refs_11_ = bf16[32,1024]{1,0:T(8,128)(2,1)S(1)} collective-permute-done((bf16[32,1024]{1,0:T(8,128)(2,1)S(1)}, bf16[32,1024]{1,0:T(8,128)(2,1)S(1)}, u32[]{:S(2)}, u32[]{:S(2)}) %collective-permute-start.15) | collective-permute-done | bytes 65568 | tf_op jit(solution)/shard_map/ppermute | solution.py:317
  58.9 6.5 %sweeps.1 = bf16[32,16,1024]{2,1,0:T(8,128)(2,1)} custom-call(s32[2]{0:T(128)S(1)} %pad_add_fusion.scal, f32[1,1024]{1,0:T(1,128)S(1)} %bitcast.12, f32[32,8,1024]{2,1,0:T(8,128)S(1)} %get-tuple-element.48.first, f32[32,8,1024]{2,1,0:T(8,128)S(1)} %get-tuple-element.49.second, f32[32,8,1024]{2,1,0:T(8,128)S(1)} %get-tuple-element.50.cross, ...), custom_call_target="tpu_custom_call" | custom-call | flops 20971520 | bytes 15728640 | tf_op jit(solution)/shard_map/sweeps/pallas_call | solution.py:284
  (5 shorter events, 0.1 us)
Async XLA Ops:
  0.0 3.3 %copy-start = (bf16[2,256,1024]{2,1,0:T(8,128)(2,1)S(1)}, bf16[2,256,1024]{2,1,0:T(8,128)(2,1)}, u32[]{:S(2)}) copy-start(bf16[2,256,1024]{2,1,0:T(8,128)(2,1)} %field.3) | copy-start | bytes 3145732
  0.0 1.8 %copy-start.6 = (bf16[3,2,1024]{2,1,0:T(2,128)(2,1)S(1)}, bf16[3,2,1024]{2,1,0:T(2,128)(2,1)}, u32[]{:S(2)}) copy-start(bf16[3,2,1024]{2,1,0:T(2,128)(2,1)} %param.9) | copy-start | bytes 36868
  0.0 3.3 %copy-start.5 = (f32[2,1024]{1,0:T(2,128)S(1)}, f32[2,1024]{1,0:T(2,128)}, u32[]{:S(2)}) copy-start(f32[2,1024]{1,0:T(2,128)} %col_c.3) | copy-start | bytes 24580
  1.2 2.1 %copy-start.2 = (bf16[256,256]{1,0:T(8,128)(2,1)S(1)}, bf16[256,256]{1,0:T(8,128)(2,1)}, u32[]{:S(2)}) copy-start(bf16[256,256]{1,0:T(8,128)(2,1)} %constant.46.clone.low) | copy-start | bytes 393220
  1.2 2.1 %collective-permute-start.1 = (bf16[1,256,1024]{2,1,0:T(8,128)(2,1)S(1)}, bf16[1,256,1024]{2,1,0:T(8,128)(2,1)S(1)}, u32[]{:S(2)}, u32[]{:S(2)}) collective-permute-start(bf16[1,256,1024]{2,1,0:T(8,128)(2,1)S(1)} %constant_dynamic-slice_fusion), channel_id=1, source_target_pairs={{0,1},{1,0},{2,3},{3,2},{4,5},{5,4},{6,7},{7,6},{8,9},{9,8},{10,11... | collective-permute-start | bytes 1572872 | tf_op jit(solution)/shard_map/ppermute | solution.py:317
  1.9 1.4 %copy-start.4 = (f32[1024]{0:T(1024)S(1)}, f32[1024]{0:T(1024)}, u32[]{:S(2)}) copy-start(f32[1024]{0:T(1024)} %param.11) | copy-start | bytes 12292
  3.3 1.2 %copy-start.1 = (bf16[2,256,1024]{2,1,0:T(8,128)(2,1)S(1)}, bf16[2,256,1024]{2,1,0:T(8,128)(2,1)}, u32[]{:S(2)}) copy-start(bf16[2,256,1024]{2,1,0:T(8,128)(2,1)} %source.3) | copy-start | bytes 3145732
  4.5 0.9 %copy-start.3 = (bf16[256,256]{1,0:T(8,128)(2,1)S(1)}, bf16[256,256]{1,0:T(8,128)(2,1)}, u32[]{:S(2)}) copy-start(bf16[256,256]{1,0:T(8,128)(2,1)} %constant.45.clone.high) | copy-start | bytes 393220
  8.4 12.7 %collective-permute-start.3 = (bf16[1,256,1024]{2,1,0:T(8,128)(2,1)S(1)}, bf16[1,256,1024]{2,1,0:T(8,128)(2,1)S(1)}, u32[]{:S(2)}, u32[]{:S(2)}) collective-permute-start(bf16[1,256,1024]{2,1,0:T(8,128)(2,1)S(1)} %get-tuple-element.33), channel_id=1, source_target_pairs={{0,15},{1,2},{2,1},{3,4},{4,3},{5,6},{6,5},{7,8},{8,7},{9,10},{10,... | collective-permute-start | bytes 1572872 | tf_op jit(solution)/shard_map/ppermute | solution.py:317
  14.2 14.1 %collective-permute-start.2 = (bf16[8,16,1024]{2,1,0:T(8,128)(2,1)S(1)}, bf16[8,16,1024]{2,1,0:T(8,128)(2,1)S(1)}, u32[]{:S(2)}, u32[]{:S(2)}) collective-permute-start(bf16[8,16,1024]{2,1,0:T(8,128)(2,1)S(1)} %get-tuple-element.32), channel_id=1, source_target_pairs={{0,1},{1,0},{2,3},{3,2},{4,5},{5,4},{6,7},{7,6},{8,9},{9,8},{10,11... | collective-permute-start | bytes 786440 | tf_op jit(solution)/shard_map/ppermute | solution.py:317
  24.1 7.1 %collective-permute-start.4 = (bf16[8,16,1024]{2,1,0:T(8,128)(2,1)S(1)}, bf16[8,16,1024]{2,1,0:T(8,128)(2,1)S(1)}, u32[]{:S(2)}, u32[]{:S(2)}) collective-permute-start(bf16[8,16,1024]{2,1,0:T(8,128)(2,1)S(1)} %get-tuple-element.35), channel_id=1, source_target_pairs={{0,1},{1,0},{2,3},{3,2},{4,5},{5,4},{6,7},{7,6},{8,9},{9,8},{10,11... | collective-permute-start | bytes 786440 | tf_op jit(solution)/shard_map/ppermute | solution.py:317
  27.1 1.2 %collective-permute-start = (f32[2,1024]{1,0:T(2,128)S(1)}, f32[2,1024]{1,0:T(2,128)S(1)}, u32[]{:S(2)}, u32[]{:S(2)}) collective-permute-start(f32[2,1024]{1,0:T(2,128)S(1)} %copy-done.5), channel_id=1, source_target_pairs={{0,1},{1,0},{2,3},{3,2},{4,5},{5,4},{6,7},{7,6},{8,9},{9,8},{10,11... | collective-permute-start | bytes 24584 | tf_op jit(solution)/shard_map/ppermute | solution.py:317
  28.3 8.9 %collective-permute-start.8 = (bf16[40,1024]{1,0:T(8,128)(2,1)S(1)}, bf16[40,1024]{1,0:T(8,128)(2,1)S(1)}, u32[]{:S(2)}, u32[]{:S(2)}) collective-permute-start(bf16[40,1024]{1,0:T(8,128)(2,1)S(1)} %get-tuple-element.39), channel_id=1, source_target_pairs={{0,8},{1,9},{2,10},{3,11},{4,12},{5,13},{6,14},{7,15},{8,0},{9,1},... | collective-permute-start | bytes 245768 | tf_op jit(solution)/shard_map/ppermute | solution.py:317
  31.2 19.3 %collective-permute-start.5 = (bf16[72,1024]{1,0:T(8,128)(2,1)S(1)}, bf16[72,1024]{1,0:T(8,128)(2,1)S(1)}, u32[]{:S(2)}, u32[]{:S(2)}) collective-permute-start(bf16[72,1024]{1,0:T(8,128)(2,1)S(1)} %get-tuple-element.36), channel_id=1, source_target_pairs={{0,2},{1,3},{2,0},{3,1},{4,6},{5,7},{6,4},{7,5},{8,10},{9,11},{10,... | collective-permute-start | bytes 442376 | tf_op jit(solution)/shard_map/ppermute | solution.py:317
  33.1 18.8 %collective-permute-start.6 = (bf16[72,1024]{1,0:T(8,128)(2,1)S(1)}, bf16[72,1024]{1,0:T(8,128)(2,1)S(1)}, u32[]{:S(2)}, u32[]{:S(2)}) collective-permute-start(bf16[72,1024]{1,0:T(8,128)(2,1)S(1)} %get-tuple-element.37), channel_id=1, source_target_pairs={{0,4},{1,5},{2,6},{3,7},{4,0},{5,1},{6,2},{7,3},{8,12},{9,13},{10,... | collective-permute-start | bytes 442376 | tf_op jit(solution)/shard_map/ppermute | solution.py:317
  34.7 11.6 %collective-permute-start.9 = (bf16[40,1024]{1,0:T(8,128)(2,1)S(1)}, bf16[40,1024]{1,0:T(8,128)(2,1)S(1)}, u32[]{:S(2)}, u32[]{:S(2)}) collective-permute-start(bf16[40,1024]{1,0:T(8,128)(2,1)S(1)} %get-tuple-element.40), channel_id=1, source_target_pairs={{0,10},{1,11},{2,8},{3,9},{4,14},{5,15},{6,12},{7,13},{8,2},{9,3},... | collective-permute-start | bytes 245768 | tf_op jit(solution)/shard_map/ppermute | solution.py:317
  34.7 11.6 %collective-permute-start.10 = (bf16[40,1024]{1,0:T(8,128)(2,1)S(1)}, bf16[40,1024]{1,0:T(8,128)(2,1)S(1)}, u32[]{:S(2)}, u32[]{:S(2)}) collective-permute-start(bf16[40,1024]{1,0:T(8,128)(2,1)S(1)} %get-tuple-element.41), channel_id=1, source_target_pairs={{0,12},{1,13},{2,14},{3,15},{4,8},{5,9},{6,10},{7,11},{8,4},{9,5},... | collective-permute-start | bytes 245768 | tf_op jit(solution)/shard_map/ppermute | solution.py:317
  37.2 10.3 %collective-permute-start.11 = (bf16[40,1024]{1,0:T(8,128)(2,1)S(1)}, bf16[40,1024]{1,0:T(8,128)(2,1)S(1)}, u32[]{:S(2)}, u32[]{:S(2)}) collective-permute-start(bf16[40,1024]{1,0:T(8,128)(2,1)S(1)} %get-tuple-element.42), channel_id=1, source_target_pairs={{0,14},{1,15},{2,12},{3,13},{4,10},{5,11},{6,8},{7,9},{8,6},{9,7},... | collective-permute-start | bytes 245768 | tf_op jit(solution)/shard_map/ppermute | solution.py:317
  46.3 10.9 %collective-permute-start.7 = (bf16[72,1024]{1,0:T(8,128)(2,1)S(1)}, bf16[72,1024]{1,0:T(8,128)(2,1)S(1)}, u32[]{:S(2)}, u32[]{:S(2)}) collective-permute-start(bf16[72,1024]{1,0:T(8,128)(2,1)S(1)} %get-tuple-element.38), channel_id=1, source_target_pairs={{0,6},{1,7},{2,4},{3,5},{4,2},{5,3},{6,0},{7,1},{8,14},{9,15},{10,... | collective-permute-start | bytes 442376 | tf_op jit(solution)/shard_map/ppermute | solution.py:317
  46.3 11.8 %collective-permute-start.12 = (bf16[32,1024]{1,0:T(8,128)(2,1)S(1)}, bf16[32,1024]{1,0:T(8,128)(2,1)S(1)}, u32[]{:S(2)}, u32[]{:S(2)}) collective-permute-start(bf16[32,1024]{1,0:T(8,128)(2,1)S(1)} %get-tuple-element.53), channel_id=1, source_target_pairs={{0,8},{1,9},{2,10},{3,11},{4,12},{5,13},{6,14},{7,15},{8,0},{9,1},... | collective-permute-start | bytes 196616 | tf_op jit(solution)/shard_map/ppermute | solution.py:317
  47.4 8.5 %copy-start.7 = (f32[3,128]{1,0:T(4,128)S(1)}, f32[3,128]{1,0:T(4,128)}, u32[]{:S(2)}) copy-start(f32[3,128]{1,0:T(4,128)} %constant.47.clone) | copy-start | bytes 4612
  47.4 10.6 %collective-permute-start.13 = (bf16[32,1024]{1,0:T(8,128)(2,1)S(1)}, bf16[32,1024]{1,0:T(8,128)(2,1)S(1)}, u32[]{:S(2)}, u32[]{:S(2)}) collective-permute-start(bf16[32,1024]{1,0:T(8,128)(2,1)S(1)} %get-tuple-element.54), channel_id=1, source_target_pairs={{0,10},{1,11},{2,8},{3,9},{4,14},{5,15},{6,12},{7,13},{8,2},{9,3},... | collective-permute-start | bytes 196616 | tf_op jit(solution)/shard_map/ppermute | solution.py:317
  50.5 7.6 %collective-permute-start.14 = (bf16[32,1024]{1,0:T(8,128)(2,1)S(1)}, bf16[32,1024]{1,0:T(8,128)(2,1)S(1)}, u32[]{:S(2)}, u32[]{:S(2)}) collective-permute-start(bf16[32,1024]{1,0:T(8,128)(2,1)S(1)} %get-tuple-element.55), channel_id=1, source_target_pairs={{0,12},{1,13},{2,14},{3,15},{4,8},{5,9},{6,10},{7,11},{8,4},{9,5},... | collective-permute-start | bytes 196616 | tf_op jit(solution)/shard_map/ppermute | solution.py:317
  51.9 7.0 %collective-permute-start.15 = (bf16[32,1024]{1,0:T(8,128)(2,1)S(1)}, bf16[32,1024]{1,0:T(8,128)(2,1)S(1)}, u32[]{:S(2)}, u32[]{:S(2)}) collective-permute-start(bf16[32,1024]{1,0:T(8,128)(2,1)S(1)} %get-tuple-element.56), channel_id=1, source_target_pairs={{0,14},{1,15},{2,12},{3,13},{4,10},{5,11},{6,8},{7,9},{8,6},{9,7},... | collective-permute-start | bytes 196616 | tf_op jit(solution)/shard_map/ppermute | solution.py:317
